TPU v7x, 32 devices: a whole 2x2x4 slice. The times are simulated.
32 devices in a mesh: modes: 16 (over z, x, core), gz: 2 (over y).
Axes of the slice: x: 2, y: 2, z: 4, core: 2. Of those that a mesh axis runs over, the one named last changes fastest.
Arguments:
- launch_spectrum: float32 [2, 256, 16384], P(None, 'modes'), may hold values from -6 to 6
- step_phase: float32 [256, 16384], P('modes'), may hold values from -3.140625 to 3.140625
- mode_profiles: bfloat16 [2048, 256], replicated, may hold values from -0.375 to 0.375
- kerr_weights: float32 [2048], replicated, may hold values from 0.02 to 0.2
Outputs:
- spectra: float32 [2, 2, 256, 16384], P('gz', None, 'modes')
All inputs are finite; a program needn't handle non-finite values.
Results may differ from a plain program's by a relative error of at most 0.0025.
Values may be sent and summed in bfloat16 or wider, within the bound.
No kernel may reach another device: no remote copies, remote signals or barrier semaphores. Data moves between devices by JAX's collectives and lax.ppermute only.
A program may use at most 64 MiB of HBM per device.

v0:
```python
import functools
import math

import jax
import jax.numpy as jnp
import numpy as np
from jax import lax
from jax.experimental import pallas as pl
from jax.experimental.pallas import tpu as pltpu
from jax.sharding import PartitionSpec as P

RADIX = 128
STRIPES = 8
SPACES = pltpu.MemorySpace

f32 = jnp.float32
bf16 = jnp.bfloat16


def halves(table):
    high = table.astype(jnp.bfloat16)
    low = (table - high.astype(np.float64)).astype(jnp.bfloat16)
    return high, low


@functools.lru_cache(None)
def tables(length):
    radix = RADIX
    other = length // radix
    index = np.arange(radix)
    second = np.arange(other)
    scale = 1.0 / math.sqrt(length)
    angle = 2.0 * math.pi / radix * (index[:, None] * index[None, :] % radix)
    cos, sin = np.cos(angle), np.sin(angle)
    last = 2.0 * math.pi / other * (second[:, None] * second[None, :] % other)
    cos2, sin2 = np.cos(last), np.sin(last)
    turn = 2.0 * math.pi / length * (index[:, None] * second[None, :] % length)
    twist = np.stack([np.cos(turn), np.sin(turn)]).astype(np.float32)
    inv_first = np.block([[cos, -sin], [sin, cos]])
    inv_second = np.block([[cos2, sin2], [-sin2, cos2]]) * scale
    fwd_first = np.block([[sin2, cos2], [-cos2, sin2]])
    fwd_second = np.block([[cos, sin], [-sin, cos]]) * scale
    return dict(
        twist=twist,
        inv_first=halves(inv_first),
        inv_second=halves(inv_second),
        fwd_first=halves(fwd_first),
        fwd_second=halves(fwd_second),
    )


def split(values):
    high = values.astype(bf16)
    return high, (values - high.astype(f32)).astype(bf16)


def dot(left, right):
    return lax.dot_general(left, right, (((1,), (0,)), ((), ())), preferred_element_type=f32)


TWO_PI = 2.0 * math.pi
TWO_PI_HIGH = float(np.float32(6.28125))
TWO_PI_LOW = TWO_PI - TWO_PI_HIGH
SIN_TERMS = [(-1) ** n / math.factorial(2 * n + 1) for n in range(6)]
COS_TERMS = [(-1) ** n / math.factorial(2 * n) for n in range(7)]


def sincos(phase):
    turns = jnp.round(phase * (1.0 / TWO_PI))
    rest = (phase - turns * TWO_PI_HIGH) - turns * TWO_PI_LOW
    half = 0.5 * rest
    square = half * half
    sine = SIN_TERMS[-1]
    for term in SIN_TERMS[-2::-1]:
        sine = sine * square + term
    sine = sine * half
    cosine = COS_TERMS[-1]
    for term in COS_TERMS[-2::-1]:
        cosine = cosine * square + term
    twice = sine + sine
    return twice * cosine, 1.0 - twice * sine


def specs(text):
    spaces = dict(s=SPACES.SMEM, v=SPACES.VMEM, h=SPACES.HBM, a=pl.ANY)
    return [pl.BlockSpec(memory_space=spaces[letter]) for letter in text]


def params():
    return pltpu.CompilerParams(vmem_limit_bytes=48 * 1024 * 1024)


def stripe(at, length):
    width = length // STRIPES
    return slice(at * width, (at + 1) * width)


def inverse_kernel(
    modes,
    devices,
    factor,
    launch,
    phase,
    twist,
    fh,
    fl,
    sh,
    sl,
    out,
    natural,
    turned,
    launched,
    phases,
    sems,
):
    radix = RADIX
    length = launch.shape[-1]
    copies = []
    for at in range(STRIPES):
        cut = stripe(at, length)
        copies.append(
            [
                pltpu.make_async_copy(
                    launch.at[:, :, cut], launched.at[:, :, cut], sems.at[2 * at]
                ),
                pltpu.make_async_copy(phase.at[:, cut], phases.at[:, cut], sems.at[2 * at + 1]),
            ]
        )
        for copy in copies[-1]:
            copy.start()

    def rotate(k1, carry):
        at = pl.ds(pl.multiple_of(k1 * radix, radix), radix)
        rows = pl.ds(pl.multiple_of(k1 * modes, modes), modes)
        sine, cosine = sincos(phases[:, at] * factor[0, 0])
        real, imag = launched[0, :, at], launched[1, :, at]
        natural[0, rows, :] = real * cosine - imag * sine
        natural[1, rows, :] = real * sine + imag * cosine
        return carry

    for at in range(STRIPES):
        for copy in copies[at]:
            copy.wait()
        part = radix // STRIPES
        lax.fori_loop(at * part, (at + 1) * part, rotate, 0, unroll=4)
    for pair in range(modes // 2):
        both = []
        for m in (2 * pair, 2 * pair + 1):
            both.append(
                jnp.concatenate([natural[c, pl.ds(m, radix, stride=modes), :] for c in range(2)], 0)
            )
        high, low = split(jnp.concatenate(both, 1))
        section = dot(fh[...], high) + (dot(fh[...], low) + dot(fl[...], high))
        rows = []
        for side in range(2):
            real = section[:radix, side * radix : (side + 1) * radix]
            imag = section[radix:, side * radix : (side + 1) * radix]
            rows.append(
                jnp.concatenate(
                    [real * twist[0] - imag * twist[1], real * twist[1] + imag * twist[0]], 1
                )
            )
        high, low = split(jnp.concatenate(rows, 0))
        final = dot(high, sh[...]) + (dot(low, sh[...]) + dot(high, sl[...]))
        for side in range(2):
            for c in range(2):
                turned[c, pl.ds(2 * pair + side, radix, stride=modes), :] = final[
                    side * radix : (side + 1) * radix, c * radix : (c + 1) * radix
                ]
    each = radix // devices
    for t2 in range(radix):
        target, slot = divmod(t2, each)
        for c in range(2):
            out[target, c * modes : (c + 1) * modes, slot * radix : (slot + 1) * radix] = turned[
                c, t2 * modes : (t2 + 1) * modes, :
            ].astype(bf16)


def inverse(factor, launch, phase, devices):
    _, modes, length = launch.shape
    table = tables(length)
    return pl.pallas_call(
        functools.partial(inverse_kernel, modes, devices),
        out_shape=jax.ShapeDtypeStruct((devices, 2 * modes, length // devices), bf16),
        in_specs=specs("shhvvvvv"),
        out_specs=specs("v")[0],
        scratch_shapes=[
            pltpu.VMEM((2, RADIX * modes, RADIX), f32),
            pltpu.VMEM((2, RADIX * modes, RADIX), f32),
            pltpu.VMEM(launch.shape, f32),
            pltpu.VMEM(phase.shape, f32),
            pltpu.SemaphoreType.DMA((2 * STRIPES,)),
        ],
        compiler_params=params(),
        name="inverse",
    )(
        factor,
        *[
            pltpu.with_memory_space_constraint(value, SPACES.HBM)
            for value in (
                launch,
                phase,
                *map(jnp.asarray, (table["twist"], *table["inv_first"], *table["inv_second"])),
            )
        ],
    )


def kerr_kernel(modes, devices, step, me, fields, profiles, flipped, weights, *rest):
    outs, (gathered, total, sems) = rest[:devices], rest[devices:]
    points = profiles.shape[0]
    width = fields.shape[-1]
    tiles = 2
    lanes = width // tiles
    copies = []
    for tile in range(tiles):
        cut = slice(tile * lanes, (tile + 1) * lanes)
        for source in range(devices):
            for c in range(2):
                copies.append(
                    pltpu.make_async_copy(
                        fields.at[source, c * modes : (c + 1) * modes, cut],
                        gathered.at[c, source * modes : (source + 1) * modes, cut],
                        sems.at[len(copies)],
                    )
                )
                copies[-1].start()
    for tile in range(tiles):
        cut = slice(tile * lanes, (tile + 1) * lanes)
        for copy in copies[tile * 2 * devices : (tile + 1) * 2 * devices]:
            copy.wait()
        for at in range(0, points, step):
            lines = profiles[at : at + step, :]
            real = dot(lines, gathered[0, :, cut])
            imag = dot(lines, gathered[1, :, cut])
            power = weights[at : at + step, :] * (real * real + imag * imag)
            back = flipped[:, at : at + step]
            parts = [dot(back, (power * real).astype(bf16)), dot(back, (power * imag).astype(bf16))]
            if at == 0:
                total[0, :, cut], total[1, :, cut] = parts
            else:
                total[0, :, cut] += parts[0]
                total[1, :, cut] += parts[1]
    for hop in range(devices):
        rows = pl.ds(pl.multiple_of((me[0, 0] ^ hop) * modes, modes), modes)
        for c in range(2):
            outs[hop][c * modes : (c + 1) * modes, :] = total[c, rows, :].astype(bf16)


def kerr(me, fields, profiles, flipped, weights, modes):
    devices, _, width = fields.shape
    return pl.pallas_call(
        functools.partial(kerr_kernel, modes, devices, 512),
        out_shape=[jax.ShapeDtypeStruct((2 * modes, width), bf16)] * devices,
        in_specs=specs("savvv"),
        out_specs=specs("v" * devices),
        scratch_shapes=[
            pltpu.VMEM((2, devices * modes, width), bf16),
            pltpu.VMEM((2, devices * modes, width), f32),
            pltpu.SemaphoreType.DMA((4 * devices,)),
        ],
        compiler_params=params(),
        name="kerr",
    )(me, fields, profiles, flipped, weights)


def first_section(modes, block, source, each, twist, fh, fl, write):
    radix = RADIX
    rows = []
    for slot in range(each):
        at = slice(slot * radix, (slot + 1) * radix)
        rows.append(
            jnp.concatenate([block[c * modes : (c + 1) * modes, at] for c in range(2)], 1)
        )
    block = jnp.concatenate(rows, 0)
    section = dot(block, fh[...]) + dot(block, fl[...])
    for slot in range(each):
        here = slice(slot * modes, (slot + 1) * modes)
        real, imag = section[here, :radix], section[here, radix:]
        row = pl.ds(source * each + slot, 1)
        cosine, sine = twist[0, row, :], twist[1, row, :]
        write(0, slot, real * cosine + imag * sine)
        write(1, slot, imag * cosine - real * sine)


def late_kernel(modes, devices, last, me, factor, base, phase, twist, fh, fl, sh, sl, *rest):
    groups, out, (turned, final), spare = rest[:4], rest[4], rest[5:7], rest[7:]
    radix = RADIX
    each = radix // devices
    size = each * modes
    length = base.shape[-1]
    for group, hops in zip(groups, groups_of(devices)):
        for at, hop in enumerate(hops):
            source = me[0, 0] ^ hop

            def write(c, slot, values, source=source):
                rows = pl.ds(pl.multiple_of(source * size + slot * modes, modes), modes)
                turned[c, rows, :] = values

            first_section(modes, group.at[at], source, each, twist, fh, fl, write)
    for pair in range(modes // 2):
        both = []
        for m in (2 * pair, 2 * pair + 1):
            both.append(
                jnp.concatenate([turned[c, pl.ds(m, radix, stride=modes), :] for c in range(2)], 0)
            )
        high, low = split(jnp.concatenate(both, 1))
        section = dot(sh[...], high) + (dot(sh[...], low) + dot(sl[...], high))
        for side in range(2):
            for c in range(2):
                final[c, pl.ds(2 * pair + side, radix, stride=modes), :] = section[
                    c * radix : (c + 1) * radix, side * radix : (side + 1) * radix
                ]
    result = spare[0] if last else out

    def finish(k1, carry):
        at = pl.ds(pl.multiple_of(k1 * radix, radix), radix)
        rows = pl.ds(pl.multiple_of(k1 * modes, modes), modes)
        sine, cosine = sincos(phase[:, at] * factor[0, 0])
        real, imag = final[0, rows, :], final[1, rows, :]
        result[0, :, at] = base[0, :, at] + (real * cosine + imag * sine)
        result[1, :, at] = base[1, :, at] + (imag * cosine - real * sine)
        return carry

    copies = []
    for at in range(STRIPES):
        cut = stripe(at, length)
        part = radix // STRIPES
        lax.fori_loop(at * part, (at + 1) * part, finish, 0, unroll=4)
        if last:
            copies.append(
                pltpu.make_async_copy(result.at[:, :, cut], out.at[:, :, cut], spare[1].at[at])
            )
            copies[-1].start()
    for copy in copies:
        copy.wait()


def late(me, factor, groups, base, phase, devices, last):
    _, modes, length = base.shape
    table = tables(length)
    spare = [pltpu.VMEM(base.shape, f32), pltpu.SemaphoreType.DMA((STRIPES,))]
    return pl.pallas_call(
        functools.partial(late_kernel, modes, devices, last),
        out_shape=jax.ShapeDtypeStruct(base.shape, f32),
        in_specs=specs("ssvvvvvvvvvvv"),
        out_specs=specs("h" if last else "v")[0],
        scratch_shapes=[pltpu.VMEM((2, RADIX * modes, RADIX), f32)] * 2 + (spare if last else []),
        compiler_params=params(),
        name="late",
    )(
        me,
        factor,
        base,
        phase,
        table["twist"],
        *table["fwd_first"],
        *table["fwd_second"],
        *groups,
    )


def regular(modes, devices):
    return modes % 16 == 0 and devices & (devices - 1) == 0 and 4 <= devices <= RADIX


def matrix(name, length):
    high, low = tables(length)[name]
    return high.astype(np.float32) + low.astype(np.float32)


def einsum(text, left, right):
    return jnp.einsum(text, left, right, precision=lax.Precision.HIGHEST)


def inverse_plain(factor, launch, phase, devices):
    _, modes, length = launch.shape
    twist = tables(length)["twist"]
    angle = phase * factor[0, 0]
    cosine, sine = jnp.cos(angle), jnp.sin(angle)
    real = launch[0] * cosine - launch[1] * sine
    imag = launch[0] * sine + launch[1] * cosine
    both = jnp.stack([real, imag]).reshape(2, modes, RADIX, -1)
    first = matrix("inv_first", length).reshape(2, RADIX, 2, RADIX)
    real, imag = einsum("dtck,cmkj->dmtj", first, both)
    both = jnp.stack([real * twist[0] - imag * twist[1], real * twist[1] + imag * twist[0]])
    other = length // RADIX
    second = matrix("inv_second", length).reshape(2, other, 2, other)
    both = einsum("cmtj,cjdu->dmtu", both, second).astype(bf16)
    both = both.reshape(2, modes, devices, -1)
    return both.transpose(2, 0, 1, 3).reshape(devices, 2 * modes, -1)


def kerr_plain(fields, profiles, weights, modes):
    devices, _, width = fields.shape
    fields = fields.reshape(devices, 2, modes, width).swapaxes(0, 1)
    fields = fields.reshape(2, devices * modes, width)
    expanded = jnp.einsum("pm,cmt->cpt", profiles, fields, preferred_element_type=f32)
    power = weights * (expanded[0] * expanded[0] + expanded[1] * expanded[1])
    cubed = (power * expanded).astype(bf16)
    projected = jnp.einsum("pm,cpt->cmt", profiles, cubed, preferred_element_type=f32)
    projected = projected.astype(bf16).reshape(2, devices, modes, width)
    return projected.swapaxes(0, 1).reshape(devices, 2 * modes, width)


def forward_plain(factor, base, phase, piece, devices):
    _, modes, length = base.shape
    other = length // RADIX
    twist = tables(length)["twist"]
    both = piece.astype(f32).reshape(devices, 2, modes, -1, other)
    both = both.transpose(1, 2, 0, 3, 4).reshape(2, modes, RADIX, other)
    first = matrix("fwd_first", length).reshape(2, other, 2, other)
    real, imag = einsum("cmtu,cudj->dmtj", both, first)
    both = jnp.stack([real * twist[0] + imag * twist[1], imag * twist[0] - real * twist[1]])
    second = matrix("fwd_second", length).reshape(2, RADIX, 2, RADIX)
    real, imag = einsum("dkct,cmtj->dmkj", second, both).reshape(2, modes, length)
    angle = phase * factor[0, 0]
    cosine, sine = jnp.cos(angle), jnp.sin(angle)
    return base + jnp.stack([real * cosine + imag * sine, imag * cosine - real * sine])


def scalar(value, dtype=f32):
    return value.astype(dtype).reshape(1, 1)


def onward(values, points):
    held = []
    for shift in range(1, points):
        pairs = [(k, k + shift) for k in range(points - shift)]
        held.append(lax.ppermute(values, "gz", pairs))
    return held


def on_device_plain(devices, points, launch, phase, profiles, weights):
    _, modes, _ = launch.shape
    place = lax.axis_index("gz")
    exchange = functools.partial(
        lax.all_to_all, axis_name="modes", split_axis=0, concat_axis=0, tiled=True
    )
    piece = exchange(inverse_plain(scalar(place + 1), launch, phase, devices))
    piece = exchange(kerr_plain(piece, profiles, weights[:, None], modes))
    result = forward_plain(scalar(place + 1), launch, phase, piece, devices)
    for shift, held in enumerate(onward(piece, points), 1):
        result = forward_plain(scalar(place + 1 - shift), result, phase, held, devices)
    return result[None]


def groups_of(devices):
    part = devices // 4
    return [tuple(range(at * part, (at + 1) * part)) for at in range(4)]


def on_device(devices, points, launch, phase, profiles, weights):
    _, modes, _ = launch.shape
    if not regular(modes, devices):
        return on_device_plain(devices, points, launch, phase, profiles, weights)
    place = lax.axis_index("gz")
    me = lax.axis_index("modes")
    here = scalar(me, jnp.int32)
    fields = inverse(scalar(place + 1), launch, phase, devices)
    fields = lax.all_to_all(fields, "modes", 0, 0, tiled=True)
    sent = kerr(here, fields, profiles, profiles.T, weights[:, None], modes)
    got = [sent[0]]
    for hop in range(1, devices):
        pairs = [(a, a ^ hop) for a in range(devices)]
        got.append(lax.ppermute(sent[hop], "modes", pairs))
    groups = groups_of(devices)
    waiting = []
    for hops in groups:
        pieces = jnp.stack([got[hop] for hop in hops])
        waiting.append([pieces] + onward(pieces, points))
    result = launch
    for shift in range(points):
        result = late(
            here,
            scalar(place + 1 - shift),
            [held[shift] for held in waiting],
            result,
            phase,
            devices,
            shift == points - 1,
        )
    return result[None]


def solution(mesh):
    in_specs = (P(None, "modes", None), P("modes", None), P(), P())
    out_specs = P("gz", None, "modes", None)
    devices, points = mesh.shape["modes"], mesh.shape["gz"]
    body = functools.partial(on_device, devices, points)
    return jax.shard_map(body, mesh=mesh, in_specs=in_specs, out_specs=out_specs, check_vma=False)
```

profile of v0, /device:TPU:0, one launch (start us, length us, event | category | flops | bytes accessed | tf_op | source)
XLA Modules:
  0.0 112.0 jit_solution(12937854897460337307)
XLA Ops:
  0.0 8.2 %inverse.1 = bf16[16,32,1024]{2,1,0:T(8,128)(2,1)} custom-call(f32[1,1]{1,0:T(1,128)} %bitcast.2.factor, f32[2,16,16384]{2,1,0:T(8,128)} %base.1, f32[16,16384]{1,0:T(8,128)} %phase.5, f32[2,128,128]{2,1,0:T(8,128)} %constant.26.clone.twist, bf16[256,256]{1,0:T(8,128)(2,1)} %constant.27.clone.fh, bf16[256,256]{1,0:T(8,128)(2,1)} %constant.28.clone.fl, ...), custom_call_target="tpu_custom_call" | custom-call | tf_op jit(solution)/shard_map/inverse/pallas_call | solution.py:182
  8.2 0.0 copy-start.8
  8.3 0.0 copy-start.1
  8.3 7.5 %all-to-all-start = ((bf16[16,32,1024]{2,1,0:T(8,128)(2,1)}), bf16[16,32,1024]{2,1,0:T(8,128)(2,1)S(1)}, u32[]{:S(2)}, u32[]{:S(2)}) async-start(bf16[16,32,1024]{2,1,0:T(8,128)(2,1)} %inverse.1), calls=%async_computation | async-start | bytes 2097152 | tf_op jit(solution)/shard_map/all_to_all | solution.py:461
  15.8 0.4 copy.16.weights
  16.2 1.4 %copy.15 = bf16[2048,256]{0,1:T(8,128)(2,1)} copy(bf16[2048,256]{1,0:T(8,128)(2,1)S(1)} %copy-done.1) | data formatting | bytes 2097152 | tf_op args[2]
  17.6 21.1 %all-to-all-done.fields = bf16[16,32,1024]{2,1,0:T(8,128)(2,1)S(1)} async-done(((bf16[16,32,1024]{2,1,0:T(8,128)(2,1)}), bf16[16,32,1024]{2,1,0:T(8,128)(2,1)S(1)}, u32[]{:S(2)}, u32[]{:S(2)}) %all-to-all-start) | async-done | bytes 1048608 | tf_op jit(solution)/shard_map/all_to_all | solution.py:461
  38.7 1.2 %copy-done.2 = bf16[2048,256]{0,1:T(8,128)(2,1)S(1)} copy-done((bf16[2048,256]{0,1:T(8,128)(2,1)S(1)}, bf16[2048,256]{0,1:T(8,128)(2,1)}, u32[]{:S(2)}) %copy-start.2) | copy-done | bytes 1048600
  39.9 8.1 %kerr.1 = (bf16[32,1024]{1,0:T(8,128)(2,1)S(1)}, bf16[32,1024]{1,0:T(8,128)(2,1)S(1)}, bf16[32,1024]{1,0:T(8,128)(2,1)S(1)}, bf16[32,1024]{1,0:T(8,128)(2,1)S(1)...) custom-call(s32[1,1]{1,0:T(1,128)} %bitcast.me, ...), custom_call_target="tpu_custom_call" | custom-call | tf_op jit(solution)/shard_map/kerr/pallas_call | solution.py:252
  48.0 0.0 copy-start
  48.0 0.0 copy-start.3
  48.1 0.0 copy-start.4
  48.1 0.0 copy-start.5
  48.1 0.0 copy-start.6
  48.1 0.0 copy-start.7
  48.1 5.1 %collective-permute-start.7 = (bf16[32,1024]{1,0:T(8,128)(2,1)S(1)}, bf16[32,1024]{1,0:T(8,128)(2,1)S(1)}, u32[]{:S(2)}, u32[]{:S(2)}) collective-permute-start(bf16[32,1024]{1,0:T(8,128)(2,1)S(1)} %get-tuple-element.29), channel_id=1, source_target_pairs={{0,16},{2,18},{4,20},{6,22},{8,24},{10,26},{12,28},{14,30},{16,0},... | collective-permute-start | bytes 196616 | tf_op jit(solution)/shard_map/ppermute | solution.py:466
  53.3 0.9 collective-permute-start.9
  54.1 2.5 %collective-permute-start.10 = (bf16[32,1024]{1,0:T(8,128)(2,1)S(1)}, bf16[32,1024]{1,0:T(8,128)(2,1)S(1)}, u32[]{:S(2)}, u32[]{:S(2)}) collective-permute-start(bf16[32,1024]{1,0:T(8,128)(2,1)S(1)} %get-tuple-element.32), channel_id=1, source_target_pairs={{0,22},{2,20},{4,18},{6,16},{8,30},{10,28},{12,26},{14,24},{16,6},... | collective-permute-start | bytes 196616 | tf_op jit(solution)/shard_map/ppermute | solution.py:466
  56.6 0.6 collective-permute-start
  57.2 1.3 %collective-permute-done.7 = bf16[32,1024]{1,0:T(8,128)(2,1)S(1)} collective-permute-done((bf16[32,1024]{1,0:T(8,128)(2,1)S(1)}, bf16[32,1024]{1,0:T(8,128)(2,1)S(1)}, u32[]{:S(2)}, u32[]{:S(2)}) %collective-permute-start.7) | collective-permute-done | bytes 65568 | tf_op jit(solution)/shard_map/ppermute | solution.py:466
  58.5 0.0 collective-permute-start.11
  58.5 4.5 %collective-permute-done.8 = bf16[32,1024]{1,0:T(8,128)(2,1)S(1)} collective-permute-done((bf16[32,1024]{1,0:T(8,128)(2,1)S(1)}, bf16[32,1024]{1,0:T(8,128)(2,1)S(1)}, u32[]{:S(2)}, u32[]{:S(2)}) %collective-permute-start.8) | collective-permute-done | bytes 65568 | tf_op jit(solution)/shard_map/ppermute | solution.py:466
  63.0 2.6 %collective-permute-start.12 = (bf16[32,1024]{1,0:T(8,128)(2,1)S(1)}, bf16[32,1024]{1,0:T(8,128)(2,1)S(1)}, u32[]{:S(2)}, u32[]{:S(2)}) collective-permute-start(bf16[32,1024]{1,0:T(8,128)(2,1)S(1)} %get-tuple-element.34), channel_id=1, source_target_pairs={{0,26},{2,24},{4,30},{6,28},{8,18},{10,16},{12,22},{14,20},{16,10}... | collective-permute-start | bytes 196616 | tf_op jit(solution)/shard_map/ppermute | solution.py:466
  65.6 0.0 collective-permute-done.9
  65.6 2.6 %collective-permute-start.13 = (bf16[32,1024]{1,0:T(8,128)(2,1)S(1)}, bf16[32,1024]{1,0:T(8,128)(2,1)S(1)}, u32[]{:S(2)}, u32[]{:S(2)}) collective-permute-start(bf16[32,1024]{1,0:T(8,128)(2,1)S(1)} %get-tuple-element.35), channel_id=1, source_target_pairs={{0,28},{2,30},{4,24},{6,26},{8,20},{10,22},{12,16},{14,18},{16,12}... | collective-permute-start | bytes 196616 | tf_op jit(solution)/shard_map/ppermute | solution.py:466
  68.1 1.7 %collective-permute-start.14 = (bf16[32,1024]{1,0:T(8,128)(2,1)S(1)}, bf16[32,1024]{1,0:T(8,128)(2,1)S(1)}, u32[]{:S(2)}, u32[]{:S(2)}) collective-permute-start(bf16[32,1024]{1,0:T(8,128)(2,1)S(1)} %get-tuple-element.36), channel_id=1, source_target_pairs={{0,30},{2,28},{4,26},{6,24},{8,22},{10,20},{12,18},{14,16},{16,14}... | collective-permute-start | bytes 196616 | tf_op jit(solution)/shard_map/ppermute | solution.py:466
  69.9 0.5 collective-permute-start.3
  70.3 0.0 collective-permute-done.12
  70.3 1.8 %collective-permute-start.4 = (bf16[32,1024]{1,0:T(8,128)(2,1)S(1)}, bf16[32,1024]{1,0:T(8,128)(2,1)S(1)}, u32[]{:S(2)}, u32[]{:S(2)}) collective-permute-start(bf16[32,1024]{1,0:T(8,128)(2,1)S(1)} %get-tuple-element.26), channel_id=1, source_target_pairs={{0,10},{2,8},{4,14},{6,12},{8,2},{10,0},{12,6},{14,4},{16,26},{18,... | collective-permute-start | bytes 196616 | tf_op jit(solution)/shard_map/ppermute | solution.py:466
  72.2 0.4 collective-permute-done.13
  72.5 4.3 %collective-permute-start.5 = (bf16[32,1024]{1,0:T(8,128)(2,1)S(1)}, bf16[32,1024]{1,0:T(8,128)(2,1)S(1)}, u32[]{:S(2)}, u32[]{:S(2)}) collective-permute-start(bf16[32,1024]{1,0:T(8,128)(2,1)S(1)} %get-tuple-element.27), channel_id=1, source_target_pairs={{0,12},{2,14},{4,8},{6,10},{8,4},{10,6},{12,0},{14,2},{16,28},{18,... | collective-permute-start | bytes 196616 | tf_op jit(solution)/shard_map/ppermute | solution.py:466
  76.8 0.0 collective-permute-done.14
  76.9 0.7 collective-permute-start.6
  77.6 0.6 collective-permute-start.1
  78.2 1.2 %collective-permute-start.2 = (bf16[32,1024]{1,0:T(8,128)(2,1)S(1)}, bf16[32,1024]{1,0:T(8,128)(2,1)S(1)}, u32[]{:S(2)}, u32[]{:S(2)}) collective-permute-start(bf16[32,1024]{1,0:T(8,128)(2,1)S(1)} %get-tuple-element.24), channel_id=1, source_target_pairs={{0,6},{2,4},{4,2},{6,0},{8,14},{10,12},{12,10},{14,8},{16,22},{18,... | collective-permute-start | bytes 196616 | tf_op jit(solution)/shard_map/ppermute | solution.py:466
  79.4 0.1 collective-permute-done.5
  79.5 3.4 %collective-permute-start.18 = (bf16[4,32,1024]{2,1,0:T(8,128)(2,1)S(1)}, bf16[4,32,1024]{2,1,0:T(8,128)(2,1)S(1)}, u32[]{:S(2)}, u32[]{:S(2)}) collective-permute-start(bf16[4,32,1024]{2,1,0:T(8,128)(2,1)S(1)} %pad_maximum_fusion.3.rest_3_), channel_id=1, source_target_pairs={{0,1},{2,3},{4,5},{6,7},{8,9},{10,11},{12,13},{14,15},{16,17},{18,... | collective-permute-start | bytes 786440 | tf_op jit(solution)/shard_map/ppermute | solution.py:430
  82.9 0.0 collective-permute-done.6
  82.9 2.3 %collective-permute-start.17 = (bf16[4,32,1024]{2,1,0:T(8,128)(2,1)S(1)}, bf16[4,32,1024]{2,1,0:T(8,128)(2,1)S(1)}, u32[]{:S(2)}, u32[]{:S(2)}) collective-permute-start(bf16[4,32,1024]{2,1,0:T(8,128)(2,1)S(1)} %pad_maximum_fusion.2.rest_2_), channel_id=1, source_target_pairs={{0,1},{2,3},{4,5},{6,7},{8,9},{10,11},{12,13},{14,15},{16,17},{18,... | collective-permute-start | bytes 786440 | tf_op jit(solution)/shard_map/ppermute | solution.py:430
  85.3 1.3 %collective-permute-start.16 = (bf16[4,32,1024]{2,1,0:T(8,128)(2,1)S(1)}, bf16[4,32,1024]{2,1,0:T(8,128)(2,1)S(1)}, u32[]{:S(2)}, u32[]{:S(2)}) collective-permute-start(bf16[4,32,1024]{2,1,0:T(8,128)(2,1)S(1)} %pad_maximum_fusion.1.rest_1_), channel_id=1, source_target_pairs={{0,1},{2,3},{4,5},{6,7},{8,9},{10,11},{12,13},{14,15},{16,17},{18,... | collective-permute-start | bytes 786440 | tf_op jit(solution)/shard_map/ppermute | solution.py:430
  86.6 0.0 collective-permute-done.1
  86.6 0.0 collective-permute-done.2
  86.7 2.0 %collective-permute-start.15 = (bf16[4,32,1024]{2,1,0:T(8,128)(2,1)S(1)}, bf16[4,32,1024]{2,1,0:T(8,128)(2,1)}, u32[]{:S(2)}, u32[]{:S(2)}) collective-permute-start(bf16[4,32,1024]{2,1,0:T(8,128)(2,1)S(1)} %pad_maximum_fusion.rest_0_), channel_id=1, source_target_pairs={{0,1},{2,3},{4,5},{6,7},{8,9},{10,11},{12,13},{14,15},{16,17},{18,... | collective-permute-start | bytes 786440 | tf_op jit(solution)/shard_map/ppermute | solution.py:430
  88.7 6.0 %late.2.base = f32[2,16,16384]{2,1,0:T(8,128)S(1)} custom-call(s32[1,1]{1,0:T(1,128)} %bitcast.me, f32[1,1]{1,0:T(1,128)} %bitcast.2.factor, f32[2,16,16384]{2,1,0:T(8,128)} %base.1, f32[16,16384]{1,0:T(8,128)S(1)} %copy-done, f32[2,128,128]{2,1,0:T(8,128)S(1)} %copy-done.5, bf16[256,256]{1,0:T(8,128)(2,1)S(1)} %copy-done.7, bf16[256,256]{1,0:T(8,128)(2,1)S(1)} %copy-done.6, ...), custom_call_target="tpu_custom_call" | custom-call | tf_op jit(solution)/shard_map/late/pallas_call | solution.py:343
  94.7 0.5 collective-permute-done.17.rest_2_
  95.2 5.6 %collective-permute-done.16.rest_1_ = bf16[4,32,1024]{2,1,0:T(8,128)(2,1)S(1)} collective-permute-done((bf16[4,32,1024]{2,1,0:T(8,128)(2,1)S(1)}, bf16[4,32,1024]{2,1,0:T(8,128)(2,1)S(1)}, u32[]{:S(2)}, u32[]{:S(2)}) %collective-permute-start.16) | collective-permute-done | bytes 262176 | tf_op jit(solution)/shard_map/ppermute | solution.py:430
  100.8 5.0 %collective-permute-done.15.rest_0_ = bf16[4,32,1024]{2,1,0:T(8,128)(2,1)} collective-permute-done((bf16[4,32,1024]{2,1,0:T(8,128)(2,1)S(1)}, bf16[4,32,1024]{2,1,0:T(8,128)(2,1)}, u32[]{:S(2)}, u32[]{:S(2)}) %collective-permute-start.15) | collective-permute-done | bytes 262176 | tf_op jit(solution)/shard_map/ppermute | solution.py:430
  105.8 6.1 %late.3 = f32[2,16,16384]{2,1,0:T(8,128)} custom-call(s32[1,1]{1,0:T(1,128)} %bitcast.me, f32[1,1]{1,0:T(1,128)} %bitcast.1.factor, f32[2,16,16384]{2,1,0:T(8,128)S(1)} %late.2.base, f32[16,16384]{1,0:T(8,128)S(1)} %copy-done, f32[2,128,128]{2,1,0:T(8,128)S(1)} %copy-done.5, bf16[256,256]{1,0:T(8,128)(2,1)S(1)} %copy-done.7, bf16[256,256]{1,0:T(8,128)(2,1)S(1)} %copy-done.6, ...), custom_call_target="tpu_custom_call" | custom-call | tf_op jit(solution)/shard_map/late/pallas_call | solution.py:343
  (20 shorter events, 0.2 us)
Async XLA Ops:
  8.2 7.6 %copy-start.8 = (f32[2048]{0:T(1024)S(1)}, f32[2048]{0:T(1024)}, u32[]{:S(2)}) copy-start(f32[2048]{0:T(1024)} %param.16) | copy-start | bytes 24580
  8.3 7.9 %copy-start.1 = (bf16[2048,256]{1,0:T(8,128)(2,1)S(1)}, bf16[2048,256]{1,0:T(8,128)(2,1)}, u32[]{:S(2)}) copy-start(bf16[2048,256]{1,0:T(8,128)(2,1)} %profiles.1) | copy-start | bytes 3145732
  8.3 30.4 %all-to-all-start = ((bf16[16,32,1024]{2,1,0:T(8,128)(2,1)}), bf16[16,32,1024]{2,1,0:T(8,128)(2,1)S(1)}, u32[]{:S(2)}, u32[]{:S(2)}) async-start(bf16[16,32,1024]{2,1,0:T(8,128)(2,1)} %inverse.1), calls=%async_computation | async-start | bytes 2097152 | tf_op jit(solution)/shard_map/all_to_all | solution.py:461
  38.7 1.2 %copy-start.2 = (bf16[2048,256]{0,1:T(8,128)(2,1)S(1)}, bf16[2048,256]{0,1:T(8,128)(2,1)}, u32[]{:S(2)}) copy-start(bf16[2048,256]{0,1:T(8,128)(2,1)} %copy.15) | copy-start | bytes 3145732
  48.0 40.7 %copy-start = (f32[16,16384]{1,0:T(8,128)S(1)}, f32[16,16384]{1,0:T(8,128)}, u32[]{:S(2)}) copy-start(f32[16,16384]{1,0:T(8,128)} %phase.5) | copy-start | bytes 3145732
  48.0 40.6 %copy-start.3 = (bf16[256,256]{1,0:T(8,128)(2,1)S(1)}, bf16[256,256]{1,0:T(8,128)(2,1)}, u32[]{:S(2)}) copy-start(bf16[256,256]{1,0:T(8,128)(2,1)} %constant.30.clone.sl) | copy-start | bytes 393220
  48.1 40.6 %copy-start.4 = (bf16[256,256]{1,0:T(8,128)(2,1)S(1)}, bf16[256,256]{1,0:T(8,128)(2,1)}, u32[]{:S(2)}) copy-start(bf16[256,256]{1,0:T(8,128)(2,1)} %constant.29.clone.sh) | copy-start | bytes 393220
  48.1 40.6 %copy-start.5 = (f32[2,128,128]{2,1,0:T(8,128)S(1)}, f32[2,128,128]{2,1,0:T(8,128)}, u32[]{:S(2)}) copy-start(f32[2,128,128]{2,1,0:T(8,128)} %constant.26.clone.twist) | copy-start | bytes 393220
  48.1 40.6 %copy-start.6 = (bf16[256,256]{1,0:T(8,128)(2,1)S(1)}, bf16[256,256]{1,0:T(8,128)(2,1)}, u32[]{:S(2)}) copy-start(bf16[256,256]{1,0:T(8,128)(2,1)} %constant.32.clone.fl) | copy-start | bytes 393220
  48.1 40.6 %copy-start.7 = (bf16[256,256]{1,0:T(8,128)(2,1)S(1)}, bf16[256,256]{1,0:T(8,128)(2,1)}, u32[]{:S(2)}) copy-start(bf16[256,256]{1,0:T(8,128)(2,1)} %constant.31.clone.fh) | copy-start | bytes 393220
  48.1 10.4 %collective-permute-start.7 = (bf16[32,1024]{1,0:T(8,128)(2,1)S(1)}, bf16[32,1024]{1,0:T(8,128)(2,1)S(1)}, u32[]{:S(2)}, u32[]{:S(2)}) collective-permute-start(bf16[32,1024]{1,0:T(8,128)(2,1)S(1)} %get-tuple-element.29), channel_id=1, source_target_pairs={{0,16},{2,18},{4,20},{6,22},{8,24},{10,26},{12,28},{14,30},{16,0},... | collective-permute-start | bytes 196616 | tf_op jit(solution)/shard_map/ppermute | solution.py:466
  53.3 9.7 %collective-permute-start.8 = (bf16[32,1024]{1,0:T(8,128)(2,1)S(1)}, bf16[32,1024]{1,0:T(8,128)(2,1)S(1)}, u32[]{:S(2)}, u32[]{:S(2)}) collective-permute-start(bf16[32,1024]{1,0:T(8,128)(2,1)S(1)} %get-tuple-element.30), channel_id=1, source_target_pairs={{0,18},{2,16},{4,22},{6,20},{8,26},{10,24},{12,30},{14,28},{16,2},... | collective-permute-start | bytes 196616 | tf_op jit(solution)/shard_map/ppermute | solution.py:466
  53.3 12.3 %collective-permute-start.9 = (bf16[32,1024]{1,0:T(8,128)(2,1)S(1)}, bf16[32,1024]{1,0:T(8,128)(2,1)S(1)}, u32[]{:S(2)}, u32[]{:S(2)}) collective-permute-start(bf16[32,1024]{1,0:T(8,128)(2,1)S(1)} %get-tuple-element.31), channel_id=1, source_target_pairs={{0,20},{2,22},{4,16},{6,18},{8,28},{10,30},{12,24},{14,26},{16,4},... | collective-permute-start | bytes 196616 | tf_op jit(solution)/shard_map/ppermute | solution.py:466
  54.1 14.0 %collective-permute-start.10 = (bf16[32,1024]{1,0:T(8,128)(2,1)S(1)}, bf16[32,1024]{1,0:T(8,128)(2,1)S(1)}, u32[]{:S(2)}, u32[]{:S(2)}) collective-permute-start(bf16[32,1024]{1,0:T(8,128)(2,1)S(1)} %get-tuple-element.32), channel_id=1, source_target_pairs={{0,22},{2,20},{4,18},{6,16},{8,30},{10,28},{12,26},{14,24},{16,6},... | collective-permute-start | bytes 196616 | tf_op jit(solution)/shard_map/ppermute | solution.py:466
  56.6 28.7 %collective-permute-start = (bf16[32,1024]{1,0:T(8,128)(2,1)S(1)}, bf16[32,1024]{1,0:T(8,128)(2,1)S(1)}, u32[]{:S(2)}, u32[]{:S(2)}) collective-permute-start(bf16[32,1024]{1,0:T(8,128)(2,1)S(1)} %get-tuple-element.22), channel_id=1, source_target_pairs={{0,2},{2,0},{4,6},{6,4},{8,10},{10,8},{12,14},{14,12},{16,18},{18,... | collective-permute-start | bytes 196616 | tf_op jit(solution)/shard_map/ppermute | solution.py:466
  58.5 11.3 %collective-permute-start.11 = (bf16[32,1024]{1,0:T(8,128)(2,1)S(1)}, bf16[32,1024]{1,0:T(8,128)(2,1)S(1)}, u32[]{:S(2)}, u32[]{:S(2)}) collective-permute-start(bf16[32,1024]{1,0:T(8,128)(2,1)S(1)} %get-tuple-element.33), channel_id=1, source_target_pairs={{0,24},{2,26},{4,28},{6,30},{8,16},{10,18},{12,20},{14,22},{16,8},... | collective-permute-start | bytes 196616 | tf_op jit(solution)/shard_map/ppermute | solution.py:466
  63.0 7.3 %collective-permute-start.12 = (bf16[32,1024]{1,0:T(8,128)(2,1)S(1)}, bf16[32,1024]{1,0:T(8,128)(2,1)S(1)}, u32[]{:S(2)}, u32[]{:S(2)}) collective-permute-start(bf16[32,1024]{1,0:T(8,128)(2,1)S(1)} %get-tuple-element.34), channel_id=1, source_target_pairs={{0,26},{2,24},{4,30},{6,28},{8,18},{10,16},{12,22},{14,20},{16,10}... | collective-permute-start | bytes 196616 | tf_op jit(solution)/shard_map/ppermute | solution.py:466
  65.6 7.0 %collective-permute-start.13 = (bf16[32,1024]{1,0:T(8,128)(2,1)S(1)}, bf16[32,1024]{1,0:T(8,128)(2,1)S(1)}, u32[]{:S(2)}, u32[]{:S(2)}) collective-permute-start(bf16[32,1024]{1,0:T(8,128)(2,1)S(1)} %get-tuple-element.35), channel_id=1, source_target_pairs={{0,28},{2,30},{4,24},{6,26},{8,20},{10,22},{12,16},{14,18},{16,12}... | collective-permute-start | bytes 196616 | tf_op jit(solution)/shard_map/ppermute | solution.py:466
  68.1 8.7 %collective-permute-start.14 = (bf16[32,1024]{1,0:T(8,128)(2,1)S(1)}, bf16[32,1024]{1,0:T(8,128)(2,1)S(1)}, u32[]{:S(2)}, u32[]{:S(2)}) collective-permute-start(bf16[32,1024]{1,0:T(8,128)(2,1)S(1)} %get-tuple-element.36), channel_id=1, source_target_pairs={{0,30},{2,28},{4,26},{6,24},{8,22},{10,20},{12,18},{14,16},{16,14}... | collective-permute-start | bytes 196616 | tf_op jit(solution)/shard_map/ppermute | solution.py:466
  69.9 7.7 %collective-permute-start.3 = (bf16[32,1024]{1,0:T(8,128)(2,1)S(1)}, bf16[32,1024]{1,0:T(8,128)(2,1)S(1)}, u32[]{:S(2)}, u32[]{:S(2)}) collective-permute-start(bf16[32,1024]{1,0:T(8,128)(2,1)S(1)} %get-tuple-element.25), channel_id=1, source_target_pairs={{0,8},{2,10},{4,12},{6,14},{8,0},{10,2},{12,4},{14,6},{16,24},{18,... | collective-permute-start | bytes 196616 | tf_op jit(solution)/shard_map/ppermute | solution.py:466
  70.3 7.8 %collective-permute-start.4 = (bf16[32,1024]{1,0:T(8,128)(2,1)S(1)}, bf16[32,1024]{1,0:T(8,128)(2,1)S(1)}, u32[]{:S(2)}, u32[]{:S(2)}) collective-permute-start(bf16[32,1024]{1,0:T(8,128)(2,1)S(1)} %get-tuple-element.26), channel_id=1, source_target_pairs={{0,10},{2,8},{4,14},{6,12},{8,2},{10,0},{12,6},{14,4},{16,26},{18,... | collective-permute-start | bytes 196616 | tf_op jit(solution)/shard_map/ppermute | solution.py:466
  72.5 6.9 %collective-permute-start.5 = (bf16[32,1024]{1,0:T(8,128)(2,1)S(1)}, bf16[32,1024]{1,0:T(8,128)(2,1)S(1)}, u32[]{:S(2)}, u32[]{:S(2)}) collective-permute-start(bf16[32,1024]{1,0:T(8,128)(2,1)S(1)} %get-tuple-element.27), channel_id=1, source_target_pairs={{0,12},{2,14},{4,8},{6,10},{8,4},{10,6},{12,0},{14,2},{16,28},{18,... | collective-permute-start | bytes 196616 | tf_op jit(solution)/shard_map/ppermute | solution.py:466
  76.9 6.0 %collective-permute-start.6 = (bf16[32,1024]{1,0:T(8,128)(2,1)S(1)}, bf16[32,1024]{1,0:T(8,128)(2,1)S(1)}, u32[]{:S(2)}, u32[]{:S(2)}) collective-permute-start(bf16[32,1024]{1,0:T(8,128)(2,1)S(1)} %get-tuple-element.28), channel_id=1, source_target_pairs={{0,14},{2,12},{4,10},{6,8},{8,6},{10,4},{12,2},{14,0},{16,30},{18,... | collective-permute-start | bytes 196616 | tf_op jit(solution)/shard_map/ppermute | solution.py:466
  77.6 9.0 %collective-permute-start.1 = (bf16[32,1024]{1,0:T(8,128)(2,1)S(1)}, bf16[32,1024]{1,0:T(8,128)(2,1)S(1)}, u32[]{:S(2)}, u32[]{:S(2)}) collective-permute-start(bf16[32,1024]{1,0:T(8,128)(2,1)S(1)} %get-tuple-element.23), channel_id=1, source_target_pairs={{0,4},{2,6},{4,0},{6,2},{8,12},{10,14},{12,8},{14,10},{16,20},{18,... | collective-permute-start | bytes 196616 | tf_op jit(solution)/shard_map/ppermute | solution.py:466
  78.2 8.5 %collective-permute-start.2 = (bf16[32,1024]{1,0:T(8,128)(2,1)S(1)}, bf16[32,1024]{1,0:T(8,128)(2,1)S(1)}, u32[]{:S(2)}, u32[]{:S(2)}) collective-permute-start(bf16[32,1024]{1,0:T(8,128)(2,1)S(1)} %get-tuple-element.24), channel_id=1, source_target_pairs={{0,6},{2,4},{4,2},{6,0},{8,14},{10,12},{12,10},{14,8},{16,22},{18,... | collective-permute-start | bytes 196616 | tf_op jit(solution)/shard_map/ppermute | solution.py:466
  79.5 15.2 %collective-permute-start.18 = (bf16[4,32,1024]{2,1,0:T(8,128)(2,1)S(1)}, bf16[4,32,1024]{2,1,0:T(8,128)(2,1)S(1)}, u32[]{:S(2)}, u32[]{:S(2)}) collective-permute-start(bf16[4,32,1024]{2,1,0:T(8,128)(2,1)S(1)} %pad_maximum_fusion.3.rest_3_), channel_id=1, source_target_pairs={{0,1},{2,3},{4,5},{6,7},{8,9},{10,11},{12,13},{14,15},{16,17},{18,... | collective-permute-start | bytes 786440 | tf_op jit(solution)/shard_map/ppermute | solution.py:430
  82.9 12.3 %collective-permute-start.17 = (bf16[4,32,1024]{2,1,0:T(8,128)(2,1)S(1)}, bf16[4,32,1024]{2,1,0:T(8,128)(2,1)S(1)}, u32[]{:S(2)}, u32[]{:S(2)}) collective-permute-start(bf16[4,32,1024]{2,1,0:T(8,128)(2,1)S(1)} %pad_maximum_fusion.2.rest_2_), channel_id=1, source_target_pairs={{0,1},{2,3},{4,5},{6,7},{8,9},{10,11},{12,13},{14,15},{16,17},{18,... | collective-permute-start | bytes 786440 | tf_op jit(solution)/shard_map/ppermute | solution.py:430
  85.3 15.5 %collective-permute-start.16 = (bf16[4,32,1024]{2,1,0:T(8,128)(2,1)S(1)}, bf16[4,32,1024]{2,1,0:T(8,128)(2,1)S(1)}, u32[]{:S(2)}, u32[]{:S(2)}) collective-permute-start(bf16[4,32,1024]{2,1,0:T(8,128)(2,1)S(1)} %pad_maximum_fusion.1.rest_1_), channel_id=1, source_target_pairs={{0,1},{2,3},{4,5},{6,7},{8,9},{10,11},{12,13},{14,15},{16,17},{18,... | collective-permute-start | bytes 786440 | tf_op jit(solution)/shard_map/ppermute | solution.py:430
  86.7 19.1 %collective-permute-start.15 = (bf16[4,32,1024]{2,1,0:T(8,128)(2,1)S(1)}, bf16[4,32,1024]{2,1,0:T(8,128)(2,1)}, u32[]{:S(2)}, u32[]{:S(2)}) collective-permute-start(bf16[4,32,1024]{2,1,0:T(8,128)(2,1)S(1)} %pad_maximum_fusion.rest_0_), channel_id=1, source_target_pairs={{0,1},{2,3},{4,5},{6,7},{8,9},{10,11},{12,13},{14,15},{16,17},{18,... | collective-permute-start | bytes 786440 | tf_op jit(solution)/shard_map/ppermute | solution.py:430
where the time goes:
time: 112 us
  starting transfers between devices  41.6 us (37%)
  waiting for transfers between devices  38.4 us (34%)
  Pallas kernels  28.4 us (25%)
  local copies, waits for them, and re-layouts  3.08 us (3%)
    ppermute x15, starting transfers between devices, on_device(): got.append(lax.ppermute(sent[hop], 'modes', pairs))  25 us
    all_to_all x1, waiting for transfers between devices, on_device(): fields = lax.all_to_all(fields, 'modes', 0, 0, tiled=True)  21.1 us
    pallas_call x2, Pallas kernels, late(): pl.pallas_call(functools.partial(late_kernel, modes, devices, last), out_...  12.1 us
    ppermute x4, waiting for transfers between devices, onward(): held.append(lax.ppermute(values, 'gz', pairs))  11.1 us
    ppermute x4, starting transfers between devices, onward(): held.append(lax.ppermute(values, 'gz', pairs))  9.06 us
    pallas_call x1, Pallas kernels, inverse(): pl.pallas_call(functools.partial(inverse_kernel, modes, devices), out_sha...  8.24 us
    pallas_call x1, Pallas kernels, kerr(): pl.pallas_call(functools.partial(kerr_kernel, modes, devices, 512), out_s...  8.1 us
    all_to_all x1, starting transfers between devices, on_device(): fields = lax.all_to_all(fields, 'modes', 0, 0, tiled=True)  7.53 us
  transfers between devices with their start and end apart: 20, of which 8 were waited for; matrix products, arithmetic and copies ran while one was open for 2% of the time, Pallas kernels for 5%

commit v1 on v0

--- a/solution.py
+++ b/solution.py
@@ -207,10 +207,18 @@
 
 
 def kerr_kernel(modes, devices, step, me, fields, profiles, flipped, weights, *rest):
-    outs, (gathered, total, sems) = rest[:devices], rest[devices:]
+    chips = devices // 2
+    keeps, gives, (gathered, total, spread, sems) = (
+        rest[:chips],
+        rest[chips : chips + 2],
+        rest[-4:],
+    )
     points = profiles.shape[0]
     width = fields.shape[-1]
-    tiles = 2
+    tiles = 4
+    for at in range(points // RADIX):
+        column = jnp.broadcast_to(weights[at : at + 1, :], (RADIX, RADIX)).T
+        spread[at * RADIX : (at + 1) * RADIX, :] = column
     lanes = width // tiles
     copies = []
     for tile in range(tiles):
@@ -233,7 +241,7 @@
             lines = profiles[at : at + step, :]
             real = dot(lines, gathered[0, :, cut])
             imag = dot(lines, gathered[1, :, cut])
-            power = weights[at : at + step, :] * (real * real + imag * imag)
+            power = jnp.concatenate([spread[at : at + step, :]] * (lanes // RADIX), 1) * (real * real + imag * imag)
             back = flipped[:, at : at + step]
             parts = [dot(back, (power * real).astype(bf16)), dot(back, (power * imag).astype(bf16))]
             if at == 0:
@@ -243,25 +251,50 @@
                 total[1, :, cut] += parts[1]
     for hop in range(devices):
         rows = pl.ds(pl.multiple_of((me[0, 0] ^ hop) * modes, modes), modes)
+        chip, other = divmod(hop, 2)
+        target = gives[chip // (chips // 2)].at[chip % (chips // 2)] if other else keeps[chip]
         for c in range(2):
-            outs[hop][c * modes : (c + 1) * modes, :] = total[c, rows, :].astype(bf16)
+            target[c * modes : (c + 1) * modes, :] = total[c, rows, :].astype(bf16)
 
 
 def kerr(me, fields, profiles, flipped, weights, modes):
     devices, _, width = fields.shape
+    chips = devices // 2
     return pl.pallas_call(
-        functools.partial(kerr_kernel, modes, devices, 512),
-        out_shape=[jax.ShapeDtypeStruct((2 * modes, width), bf16)] * devices,
+        functools.partial(kerr_kernel, modes, devices, 1024),
+        out_shape=[jax.ShapeDtypeStruct((2 * modes, width), bf16)] * chips
+        + [jax.ShapeDtypeStruct((chips // 2, 2 * modes, width), bf16)] * 2,
         in_specs=specs("savvv"),
-        out_specs=specs("v" * devices),
+        out_specs=specs("v" * (chips + 2)),
         scratch_shapes=[
             pltpu.VMEM((2, devices * modes, width), bf16),
             pltpu.VMEM((2, devices * modes, width), f32),
-            pltpu.SemaphoreType.DMA((4 * devices,)),
+            pltpu.VMEM((profiles.shape[0], RADIX), f32),
+            pltpu.SemaphoreType.DMA((8 * devices,)),
         ],
         compiler_params=params(),
         name="kerr",
     )(me, fields, profiles, flipped, weights)
+
+
+def pack_kernel(count, *refs):
+    keeps, got, outs = refs[:count], refs[count], refs[count + 1 :]
+    skip = got.shape[0] - count
+    for at in range(count):
+        outs[at][0] = keeps[at][...]
+        outs[at][1] = got[skip + at]
+
+
+def pack(keeps, got):
+    count = len(keeps)
+    return pl.pallas_call(
+        functools.partial(pack_kernel, count),
+        out_shape=[jax.ShapeDtypeStruct((2,) + keeps[0].shape, bf16)] * count,
+        in_specs=specs("v" * (count + 1)),
+        out_specs=specs("v" * count),
+        compiler_params=params(),
+        name="pack",
+    )(*keeps, got)
 
 
 def first_section(modes, block, source, each, twist, fh, fl, write):
@@ -284,7 +317,9 @@
 
 
 def late_kernel(modes, devices, last, me, factor, base, phase, twist, fh, fl, sh, sl, *rest):
-    groups, out, (turned, final), spare = rest[:4], rest[4], rest[5:7], rest[7:]
+    count = len(groups_of(devices))
+    groups, out, (turned, final) = rest[:count], rest[count], rest[count + 1 : count + 3]
+    spare = rest[count + 3 :]
     radix = RADIX
     each = radix // devices
     size = each * modes
@@ -343,7 +378,7 @@
     return pl.pallas_call(
         functools.partial(late_kernel, modes, devices, last),
         out_shape=jax.ShapeDtypeStruct(base.shape, f32),
-        in_specs=specs("ssvvvvvvvvvvv"),
+        in_specs=specs("ssvvvvvvv" + "v" * len(groups)),
         out_specs=specs("h" if last else "v")[0],
         scratch_shapes=[pltpu.VMEM((2, RADIX * modes, RADIX), f32)] * 2 + (spare if last else []),
         compiler_params=params(),
@@ -361,7 +396,7 @@
 
 
 def regular(modes, devices):
-    return modes % 16 == 0 and devices & (devices - 1) == 0 and 4 <= devices <= RADIX
+    return modes % 16 == 0 and devices & (devices - 1) == 0 and 8 <= devices <= RADIX
 
 
 def matrix(name, length):
@@ -445,9 +480,21 @@
     return result[None]
 
 
+def quarters(devices):
+    part = devices // 8
+    return [tuple(range(at * part, (at + 1) * part)) for at in range(4)]
+
+
+def chips_of(devices):
+    near, close, middle, far = quarters(devices)
+    return [near] + [middle] + [close] + [(chip,) for chip in far]
+
+
 def groups_of(devices):
-    part = devices // 4
-    return [tuple(range(at * part, (at + 1) * part)) for at in range(4)]
+    return [
+        tuple(2 * chip + core for chip in chips for core in range(2))
+        for chips in chips_of(devices)
+    ]
 
 
 def on_device(devices, points, launch, phase, profiles, weights):
@@ -459,15 +506,20 @@
     here = scalar(me, jnp.int32)
     fields = inverse(scalar(place + 1), launch, phase, devices)
     fields = lax.all_to_all(fields, "modes", 0, 0, tiled=True)
-    sent = kerr(here, fields, profiles, profiles.T, weights[:, None], modes)
-    got = [sent[0]]
-    for hop in range(1, devices):
-        pairs = [(a, a ^ hop) for a in range(devices)]
-        got.append(lax.ppermute(sent[hop], "modes", pairs))
-    groups = groups_of(devices)
+    sent = kerr(here, fields, profiles, profiles.T, weights.reshape(-1, RADIX), modes)
+    chips = devices // 2
+    keeps, (near, far) = sent[:chips], sent[chips:]
+    swap = [(a, a ^ 1) for a in range(devices)]
+    far = lax.ppermute(far, "modes", swap)
+    near = lax.ppermute(near, "modes", swap)
+    got = [jnp.stack([keeps[0], near[0]])]
+    got += pack(keeps[1 : chips // 2], near) + pack(keeps[chips // 2 :], far)
+    for chip in range(1, chips):
+        pairs = [(a, a ^ (2 * chip)) for a in range(devices)]
+        got[chip] = lax.ppermute(got[chip], "modes", pairs)
     waiting = []
-    for hops in groups:
-        pieces = jnp.stack([got[hop] for hop in hops])
+    for group in chips_of(devices):
+        pieces = jnp.concatenate([got[chip] for chip in group], 0)
         waiting.append([pieces] + onward(pieces, points))
     result = launch
     for shift in range(points):

time: 112 us -> 97 us (0.87)
  starting transfers between devices: 41.6 us -> 34.9 us
  waiting for transfers between devices: 38.4 us -> 32.6 us
  local copies, waits for them, and re-layouts: 3.08 us -> 0.74 us
    ppermute x15 -> x9, starting transfers between devices: 25 us -> 15.3 us  [the longest x7 14.4 us: on_device(): got[chip] = lax.ppermute(got[chip], 'modes', pairs)]
    ppermute x4 -> x5, waiting for transfers between devices: 11.1 us -> 2.12 us  [onward(): held.append(lax.ppermute(values, 'gz', pairs))]
    ppermute x4 -> x5, starting transfers between devices: 9.06 us -> 12.1 us  [onward(): held.append(lax.ppermute(values, 'gz', pairs))]
    ppermute x15 -> x9, waiting for transfers between devices: 6.27 us -> 8.29 us  [the longest x7 7.2 us: on_device(): got[chip] = lax.ppermute(got[chip], 'modes', pairs)]
    unnamed x19, local copies, waits for them, and re-layouts: 2.71 us -> 0.72 us
    all_to_all x1, waiting for transfers between devices: 21.1 us -> 22.2 us  [on_device(): fields = lax.all_to_all(fields, 'modes', 0, 0, tiled=True)]
    pallas_call x1 -> x3, Pallas kernels: 8.1 us -> 7.7 us  [the longest x1 7.64 us: kerr(): pl.pallas_call(functools.partial(kerr_kernel, modes, devices, 1024), out_...]
  transfers between devices with their start and end apart: 20 -> 15, of which waited for: 8 -> 6; matrix products, arithmetic and copies ran while one was open for 2% -> 1% of each run, Pallas kernels for 5% -> 6%
where the time goes in v1:
time: 97 us; the launch traced here: 96.7 us
  starting transfers between devices  34.9 us (36%)
  waiting for transfers between devices  32.6 us (34%)
  Pallas kernels  28 us (29%)
    all_to_all x1, waiting for transfers between devices, on_device(): fields = lax.all_to_all(fields, 'modes', 0, 0, tiled=True)  22.2 us
    ppermute x7, starting transfers between devices, on_device(): got[chip] = lax.ppermute(got[chip], 'modes', pairs)  14.4 us
    pallas_call x2, Pallas kernels, late(): pl.pallas_call(functools.partial(late_kernel, modes, devices, last), out_...  12.1 us
    ppermute x5, starting transfers between devices, onward(): held.append(lax.ppermute(values, 'gz', pairs))  12.1 us
    pallas_call x1, Pallas kernels, inverse(): pl.pallas_call(functools.partial(inverse_kernel, modes, devices), out_sha...  8.24 us
    pallas_call x1, Pallas kernels, kerr(): pl.pallas_call(functools.partial(kerr_kernel, modes, devices, 1024), out_...  7.64 us
    all_to_all x1, starting transfers between devices, on_device(): fields = lax.all_to_all(fields, 'modes', 0, 0, tiled=True)  7.53 us
    ppermute x7, waiting for transfers between devices, on_device(): got[chip] = lax.ppermute(got[chip], 'modes', pairs)  7.2 us
  transfers between devices with their start and end apart: 15, of which 6 were waited for; matrix products, arithmetic and copies ran while one was open for 1% of the time, Pallas kernels for 6%

profile of v1, /device:TPU:0, one launch (start us, length us, event | category | flops | bytes accessed | tf_op | source)
XLA Modules:
  0.0 96.7 jit_solution(9942738571300012004)
XLA Ops:
  0.0 8.2 %inverse.1 = bf16[16,32,1024]{2,1,0:T(8,128)(2,1)} custom-call(f32[1,1]{1,0:T(1,128)} %bitcast.2.factor, f32[2,16,16384]{2,1,0:T(8,128)} %base.1, f32[16,16384]{1,0:T(8,128)} %phase.5, f32[2,128,128]{2,1,0:T(8,128)} %constant.26.clone.twist, bf16[256,256]{1,0:T(8,128)(2,1)} %constant.27.clone.fh, bf16[256,256]{1,0:T(8,128)(2,1)} %constant.28.clone.fl, ...), custom_call_target="tpu_custom_call" | custom-call | tf_op jit(solution)/shard_map/inverse/pallas_call | solution.py:182
  8.2 0.0 copy-start.1
  8.3 0.0 copy-start.7
  8.3 7.5 %all-to-all-start = ((bf16[16,32,1024]{2,1,0:T(8,128)(2,1)}), bf16[16,32,1024]{2,1,0:T(8,128)(2,1)S(1)}, u32[]{:S(2)}, u32[]{:S(2)}) async-start(bf16[16,32,1024]{2,1,0:T(8,128)(2,1)} %inverse.1), calls=%async_computation | async-start | bytes 2097152 | tf_op jit(solution)/shard_map/all_to_all | solution.py:508
  15.8 0.0 copy-done.1
  15.8 0.6 copy.14
  16.5 22.2 %all-to-all-done.fields = bf16[16,32,1024]{2,1,0:T(8,128)(2,1)S(1)} async-done(((bf16[16,32,1024]{2,1,0:T(8,128)(2,1)}), bf16[16,32,1024]{2,1,0:T(8,128)(2,1)S(1)}, u32[]{:S(2)}, u32[]{:S(2)}) %all-to-all-start) | async-done | bytes 1048608 | tf_op jit(solution)/shard_map/all_to_all | solution.py:508
  38.7 0.0 copy-done.7
  38.7 7.6 %kerr.1 = (bf16[32,1024]{1,0:T(8,128)(2,1)S(1)}, bf16[32,1024]{1,0:T(8,128)(2,1)S(1)}, bf16[32,1024]{1,0:T(8,128)(2,1)S(1)}, bf16[32,1024]{1,0:T(8,128)(2,1)S(1)...) custom-call(s32[1,1]{1,0:T(1,128)} %bitcast.me, ...), custom_call_target="tpu_custom_call" | custom-call | tf_op jit(solution)/shard_map/kerr/pallas_call | solution.py:263
  46.3 0.0 copy-start
  46.4 0.0 copy-start.2
  46.4 0.0 copy-start.3
  46.4 0.0 copy-start.4
  46.4 0.0 copy-start.5
  46.4 0.0 copy-start.6
  46.4 0.8 collective-permute-start
  47.2 0.1 collective-permute-start.2
  47.3 1.1 %collective-permute-done.refs_3_ = bf16[4,32,1024]{2,1,0:T(8,128)(2,1)S(1)} collective-permute-done((bf16[4,32,1024]{2,1,0:T(8,128)(2,1)S(1)}, bf16[4,32,1024]{2,1,0:T(8,128)(2,1)S(1)}, u32[]{:S(2)}, u32[]{:S(2)}) %collective-permute-start) | collective-permute-done | bytes 262176 | tf_op jit(solution)/shard_map/ppermute | solution.py:514
  48.4 3.4 %collective-permute-start.5 = (bf16[2,32,1024]{2,1,0:T(8,128)(2,1)S(1)}, bf16[2,32,1024]{2,1,0:T(8,128)(2,1)S(1)}, u32[]{:S(2)}, u32[]{:S(2)}) collective-permute-start(bf16[2,32,1024]{2,1,0:T(8,128)(2,1)S(1)} %get-tuple-element.35), channel_id=1, source_target_pairs={{0,8},{2,10},{4,12},{6,14},{8,0},{10,2},{12,4},{14,6},{16,24},{18,... | collective-permute-start | bytes 393224 | tf_op jit(solution)/shard_map/ppermute | solution.py:519
  51.8 0.9 collective-permute-start.6
  52.7 0.6 collective-permute-start.1
  53.4 0.0 collective-permute-done.2.refs_4_
  53.4 3.4 %collective-permute-start.3 = (bf16[2,32,1024]{2,1,0:T(8,128)(2,1)S(1)}, bf16[2,32,1024]{2,1,0:T(8,128)(2,1)S(1)}, u32[]{:S(2)}, u32[]{:S(2)}) collective-permute-start(bf16[2,32,1024]{2,1,0:T(8,128)(2,1)S(1)} %get-tuple-element.33), channel_id=1, source_target_pairs={{0,16},{2,18},{4,20},{6,22},{8,24},{10,26},{12,28},{14,30},{16,0},... | collective-permute-start | bytes 393224 | tf_op jit(solution)/shard_map/ppermute | solution.py:519
  56.8 0.4 collective-permute-start.4
  57.2 0.0 collective-permute-done.5
  57.2 2.9 %collective-permute-start.7 = (bf16[2,32,1024]{2,1,0:T(8,128)(2,1)S(1)}, bf16[2,32,1024]{2,1,0:T(8,128)(2,1)S(1)}, u32[]{:S(2)}, u32[]{:S(2)}) collective-permute-start(bf16[2,32,1024]{2,1,0:T(8,128)(2,1)S(1)} %get-tuple-element.37), channel_id=1, source_target_pairs={{0,24},{2,26},{4,28},{6,30},{8,16},{10,18},{12,20},{14,22},{16,8},... | collective-permute-start | bytes 393224 | tf_op jit(solution)/shard_map/ppermute | solution.py:519
  60.2 2.2 %collective-permute-done.6 = bf16[2,32,1024]{2,1,0:T(8,128)(2,1)S(1)} collective-permute-done((bf16[2,32,1024]{2,1,0:T(8,128)(2,1)S(1)}, bf16[2,32,1024]{2,1,0:T(8,128)(2,1)S(1)}, u32[]{:S(2)}, u32[]{:S(2)}) %collective-permute-start.6) | collective-permute-done | bytes 131104 | tf_op jit(solution)/shard_map/ppermute | solution.py:519
  62.4 2.7 %collective-permute-start.8 = (bf16[2,32,1024]{2,1,0:T(8,128)(2,1)S(1)}, bf16[2,32,1024]{2,1,0:T(8,128)(2,1)S(1)}, u32[]{:S(2)}, u32[]{:S(2)}) collective-permute-start(bf16[2,32,1024]{2,1,0:T(8,128)(2,1)S(1)} %get-tuple-element.38), channel_id=1, source_target_pairs={{0,28},{2,30},{4,24},{6,26},{8,20},{10,22},{12,16},{14,18},{16,12}... | collective-permute-start | bytes 393224 | tf_op jit(solution)/shard_map/ppermute | solution.py:519
  65.1 0.0 collective-permute-done.1
  65.1 3.4 %collective-permute-start.11 = (bf16[4,32,1024]{2,1,0:T(8,128)(2,1)S(1)}, bf16[4,32,1024]{2,1,0:T(8,128)(2,1)S(1)}, u32[]{:S(2)}, u32[]{:S(2)}) collective-permute-start(bf16[4,32,1024]{2,1,0:T(8,128)(2,1)S(1)} %constant_dynamic-update-slice_fusion.2.rest_2_), channel_id=1, source_target_pairs={{0,1},{2,3},{4,5},{6,7},{8,9},{10,11},{12,13},{14,15},{16,17},{18,... | collective-permute-start | bytes 786440 | tf_op jit(solution)/shard_map/ppermute | solution.py:465
  68.6 0.0 collective-permute-done.3
  68.6 1.3 %collective-permute-start.9 = (bf16[4,32,1024]{2,1,0:T(8,128)(2,1)S(1)}, bf16[4,32,1024]{2,1,0:T(8,128)(2,1)S(1)}, u32[]{:S(2)}, u32[]{:S(2)}) collective-permute-start(bf16[4,32,1024]{2,1,0:T(8,128)(2,1)S(1)} %pad_maximum_fusion.rest_0_), channel_id=1, source_target_pairs={{0,1},{2,3},{4,5},{6,7},{8,9},{10,11},{12,13},{14,15},{16,17},{18,... | collective-permute-start | bytes 786440 | tf_op jit(solution)/shard_map/ppermute | solution.py:465
  69.9 5.0 %collective-permute-done.4 = bf16[2,32,1024]{2,1,0:T(8,128)(2,1)S(1)} collective-permute-done((bf16[2,32,1024]{2,1,0:T(8,128)(2,1)S(1)}, bf16[2,32,1024]{2,1,0:T(8,128)(2,1)S(1)}, u32[]{:S(2)}, u32[]{:S(2)}) %collective-permute-start.4) | collective-permute-done | bytes 131104 | tf_op jit(solution)/shard_map/ppermute | solution.py:519
  74.9 3.4 %collective-permute-start.10 = (bf16[4,32,1024]{2,1,0:T(8,128)(2,1)S(1)}, bf16[4,32,1024]{2,1,0:T(8,128)(2,1)S(1)}, u32[]{:S(2)}, u32[]{:S(2)}) collective-permute-start(bf16[4,32,1024]{2,1,0:T(8,128)(2,1)S(1)} %constant_dynamic-update-slice_fusion.rest_1_), channel_id=1, source_target_pairs={{0,1},{2,3},{4,5},{6,7},{8,9},{10,11},{12,13},{14,15},{16,17},{18,... | collective-permute-start | bytes 786440 | tf_op jit(solution)/shard_map/ppermute | solution.py:465
  78.4 0.0 collective-permute-done.7.rest_3_
  78.4 2.0 %collective-permute-start.12 = (bf16[2,32,1024]{2,1,0:T(8,128)(2,1)S(1)}, bf16[2,32,1024]{2,1,0:T(8,128)(2,1)}, u32[]{:S(2)}, u32[]{:S(2)}) collective-permute-start(bf16[2,32,1024]{2,1,0:T(8,128)(2,1)S(1)} %collective-permute-done.7.rest_3_), channel_id=1, source_target_pairs={{0,1},{2,3},{4,5},{6,7},{8,9},{10,11},{12,13},{14,15},{16,17},{18,... | collective-permute-start | bytes 393224 | tf_op jit(solution)/shard_map/ppermute | solution.py:465
  80.3 0.0 collective-permute-done.8.rest_4_
  80.3 1.9 %collective-permute-start.13 = (bf16[2,32,1024]{2,1,0:T(8,128)(2,1)S(1)}, bf16[2,32,1024]{2,1,0:T(8,128)(2,1)}, u32[]{:S(2)}, u32[]{:S(2)}) collective-permute-start(bf16[2,32,1024]{2,1,0:T(8,128)(2,1)S(1)} %collective-permute-done.8.rest_4_), channel_id=1, source_target_pairs={{0,1},{2,3},{4,5},{6,7},{8,9},{10,11},{12,13},{14,15},{16,17},{18,... | collective-permute-start | bytes 393224 | tf_op jit(solution)/shard_map/ppermute | solution.py:465
  82.3 0.0 copy-done.4
  82.3 0.0 copy-done.5
  82.3 0.0 copy-done.6
  82.3 6.0 %late.2.base = f32[2,16,16384]{2,1,0:T(8,128)S(1)} custom-call(s32[1,1]{1,0:T(1,128)} %bitcast.me, f32[1,1]{1,0:T(1,128)} %bitcast.2.factor, f32[2,16,16384]{2,1,0:T(8,128)} %base.1, f32[16,16384]{1,0:T(8,128)S(1)} %copy-done, f32[2,128,128]{2,1,0:T(8,128)S(1)} %copy-done.4, bf16[256,256]{1,0:T(8,128)(2,1)S(1)} %copy-done.6, bf16[256,256]{1,0:T(8,128)(2,1)S(1)} %copy-done.5, ...), custom_call_target="tpu_custom_call" | custom-call | tf_op jit(solution)/shard_map/late/pallas_call | solution.py:378
  88.3 0.7 collective-permute-done.12.rest_3_
  89.0 1.4 %collective-permute-done.13.rest_4_ = bf16[2,32,1024]{2,1,0:T(8,128)(2,1)} collective-permute-done((bf16[2,32,1024]{2,1,0:T(8,128)(2,1)S(1)}, bf16[2,32,1024]{2,1,0:T(8,128)(2,1)}, u32[]{:S(2)}, u32[]{:S(2)}) %collective-permute-start.13) | collective-permute-done | bytes 131104 | tf_op jit(solution)/shard_map/ppermute | solution.py:465
  90.4 0.0 collective-permute-done.11.rest_2_
  90.4 0.0 collective-permute-done.9.rest_0_
  90.4 0.0 collective-permute-done.10.rest_1_
  90.4 6.1 %late.3 = f32[2,16,16384]{2,1,0:T(8,128)} custom-call(s32[1,1]{1,0:T(1,128)} %bitcast.me, f32[1,1]{1,0:T(1,128)} %bitcast.1.factor, f32[2,16,16384]{2,1,0:T(8,128)S(1)} %late.2.base, f32[16,16384]{1,0:T(8,128)S(1)} %copy-done, f32[2,128,128]{2,1,0:T(8,128)S(1)} %copy-done.4, bf16[256,256]{1,0:T(8,128)(2,1)S(1)} %copy-done.6, bf16[256,256]{1,0:T(8,128)(2,1)S(1)} %copy-done.5, ...), custom_call_target="tpu_custom_call" | custom-call | tf_op jit(solution)/shard_map/late/pallas_call | solution.py:378
  (11 shorter events, 0.1 us)
Async XLA Ops:
  8.2 7.6 %copy-start.1 = (bf16[2048,256]{1,0:T(8,128)(2,1)S(1)}, bf16[2048,256]{1,0:T(8,128)(2,1)}, u32[]{:S(2)}) copy-start(bf16[2048,256]{1,0:T(8,128)(2,1)} %profiles.1) | copy-start | bytes 3145732
  8.3 30.4 %copy-start.7 = (f32[2048]{0:T(1024)S(1)}, f32[2048]{0:T(1024)}, u32[]{:S(2)}) copy-start(f32[2048]{0:T(1024)} %param.16) | copy-start | bytes 24580
  8.3 30.4 %all-to-all-start = ((bf16[16,32,1024]{2,1,0:T(8,128)(2,1)}), bf16[16,32,1024]{2,1,0:T(8,128)(2,1)S(1)}, u32[]{:S(2)}, u32[]{:S(2)}) async-start(bf16[16,32,1024]{2,1,0:T(8,128)(2,1)} %inverse.1), calls=%async_computation | async-start | bytes 2097152 | tf_op jit(solution)/shard_map/all_to_all | solution.py:508
  46.3 35.9 %copy-start = (f32[16,16384]{1,0:T(8,128)S(1)}, f32[16,16384]{1,0:T(8,128)}, u32[]{:S(2)}) copy-start(f32[16,16384]{1,0:T(8,128)} %phase.5) | copy-start | bytes 3145732
  46.4 35.9 %copy-start.2 = (bf16[256,256]{1,0:T(8,128)(2,1)S(1)}, bf16[256,256]{1,0:T(8,128)(2,1)}, u32[]{:S(2)}) copy-start(bf16[256,256]{1,0:T(8,128)(2,1)} %constant.30.clone.sl) | copy-start | bytes 393220
  46.4 35.9 %copy-start.3 = (bf16[256,256]{1,0:T(8,128)(2,1)S(1)}, bf16[256,256]{1,0:T(8,128)(2,1)}, u32[]{:S(2)}) copy-start(bf16[256,256]{1,0:T(8,128)(2,1)} %constant.29.clone.sh) | copy-start | bytes 393220
  46.4 35.9 %copy-start.4 = (f32[2,128,128]{2,1,0:T(8,128)S(1)}, f32[2,128,128]{2,1,0:T(8,128)}, u32[]{:S(2)}) copy-start(f32[2,128,128]{2,1,0:T(8,128)} %constant.26.clone.twist) | copy-start | bytes 393220
  46.4 35.9 %copy-start.5 = (bf16[256,256]{1,0:T(8,128)(2,1)S(1)}, bf16[256,256]{1,0:T(8,128)(2,1)}, u32[]{:S(2)}) copy-start(bf16[256,256]{1,0:T(8,128)(2,1)} %constant.32.clone.fl) | copy-start | bytes 393220
  46.4 35.9 %copy-start.6 = (bf16[256,256]{1,0:T(8,128)(2,1)S(1)}, bf16[256,256]{1,0:T(8,128)(2,1)}, u32[]{:S(2)}) copy-start(bf16[256,256]{1,0:T(8,128)(2,1)} %constant.31.clone.fh) | copy-start | bytes 393220
  46.4 1.9 %collective-permute-start = (bf16[4,32,1024]{2,1,0:T(8,128)(2,1)S(1)}, bf16[4,32,1024]{2,1,0:T(8,128)(2,1)S(1)}, u32[]{:S(2)}, u32[]{:S(2)}) collective-permute-start(bf16[4,32,1024]{2,1,0:T(8,128)(2,1)S(1)} %get-tuple-element.23), channel_id=1, source_target_pairs={{0,2},{2,0},{4,6},{6,4},{8,10},{10,8},{12,14},{14,12},{16,18},{18,... | collective-permute-start | bytes 786440 | tf_op jit(solution)/shard_map/ppermute | solution.py:514
  47.2 6.2 %collective-permute-start.2 = (bf16[4,32,1024]{2,1,0:T(8,128)(2,1)S(1)}, bf16[4,32,1024]{2,1,0:T(8,128)(2,1)S(1)}, u32[]{:S(2)}, u32[]{:S(2)}) collective-permute-start(bf16[4,32,1024]{2,1,0:T(8,128)(2,1)S(1)} %get-tuple-element.32), channel_id=1, source_target_pairs={{0,2},{2,0},{4,6},{6,4},{8,10},{10,8},{12,14},{14,12},{16,18},{18,... | collective-permute-start | bytes 786440 | tf_op jit(solution)/shard_map/ppermute | solution.py:513
  48.4 8.9 %collective-permute-start.5 = (bf16[2,32,1024]{2,1,0:T(8,128)(2,1)S(1)}, bf16[2,32,1024]{2,1,0:T(8,128)(2,1)S(1)}, u32[]{:S(2)}, u32[]{:S(2)}) collective-permute-start(bf16[2,32,1024]{2,1,0:T(8,128)(2,1)S(1)} %get-tuple-element.35), channel_id=1, source_target_pairs={{0,8},{2,10},{4,12},{6,14},{8,0},{10,2},{12,4},{14,6},{16,24},{18,... | collective-permute-start | bytes 393224 | tf_op jit(solution)/shard_map/ppermute | solution.py:519
  51.8 10.6 %collective-permute-start.6 = (bf16[2,32,1024]{2,1,0:T(8,128)(2,1)S(1)}, bf16[2,32,1024]{2,1,0:T(8,128)(2,1)S(1)}, u32[]{:S(2)}, u32[]{:S(2)}) collective-permute-start(bf16[2,32,1024]{2,1,0:T(8,128)(2,1)S(1)} %get-tuple-element.36), channel_id=1, source_target_pairs={{0,12},{2,14},{4,8},{6,10},{8,4},{10,6},{12,0},{14,2},{16,28},{18,... | collective-permute-start | bytes 393224 | tf_op jit(solution)/shard_map/ppermute | solution.py:519
  52.7 12.4 %collective-permute-start.1 = (bf16[2,32,1024]{2,1,0:T(8,128)(2,1)S(1)}, bf16[2,32,1024]{2,1,0:T(8,128)(2,1)S(1)}, u32[]{:S(2)}, u32[]{:S(2)}) collective-permute-start(bf16[2,32,1024]{2,1,0:T(8,128)(2,1)S(1)} %get-tuple-element.27), channel_id=1, source_target_pairs={{0,4},{2,6},{4,0},{6,2},{8,12},{10,14},{12,8},{14,10},{16,20},{18,... | collective-permute-start | bytes 393224 | tf_op jit(solution)/shard_map/ppermute | solution.py:519
  53.4 15.2 %collective-permute-start.3 = (bf16[2,32,1024]{2,1,0:T(8,128)(2,1)S(1)}, bf16[2,32,1024]{2,1,0:T(8,128)(2,1)S(1)}, u32[]{:S(2)}, u32[]{:S(2)}) collective-permute-start(bf16[2,32,1024]{2,1,0:T(8,128)(2,1)S(1)} %get-tuple-element.33), channel_id=1, source_target_pairs={{0,16},{2,18},{4,20},{6,22},{8,24},{10,26},{12,28},{14,30},{16,0},... | collective-permute-start | bytes 393224 | tf_op jit(solution)/shard_map/ppermute | solution.py:519
  56.8 18.1 %collective-permute-start.4 = (bf16[2,32,1024]{2,1,0:T(8,128)(2,1)S(1)}, bf16[2,32,1024]{2,1,0:T(8,128)(2,1)S(1)}, u32[]{:S(2)}, u32[]{:S(2)}) collective-permute-start(bf16[2,32,1024]{2,1,0:T(8,128)(2,1)S(1)} %get-tuple-element.34), channel_id=1, source_target_pairs={{0,20},{2,22},{4,16},{6,18},{8,28},{10,30},{12,24},{14,26},{16,4},... | collective-permute-start | bytes 393224 | tf_op jit(solution)/shard_map/ppermute | solution.py:519
  57.2 21.1 %collective-permute-start.7 = (bf16[2,32,1024]{2,1,0:T(8,128)(2,1)S(1)}, bf16[2,32,1024]{2,1,0:T(8,128)(2,1)S(1)}, u32[]{:S(2)}, u32[]{:S(2)}) collective-permute-start(bf16[2,32,1024]{2,1,0:T(8,128)(2,1)S(1)} %get-tuple-element.37), channel_id=1, source_target_pairs={{0,24},{2,26},{4,28},{6,30},{8,16},{10,18},{12,20},{14,22},{16,8},... | collective-permute-start | bytes 393224 | tf_op jit(solution)/shard_map/ppermute | solution.py:519
  62.4 18.0 %collective-permute-start.8 = (bf16[2,32,1024]{2,1,0:T(8,128)(2,1)S(1)}, bf16[2,32,1024]{2,1,0:T(8,128)(2,1)S(1)}, u32[]{:S(2)}, u32[]{:S(2)}) collective-permute-start(bf16[2,32,1024]{2,1,0:T(8,128)(2,1)S(1)} %get-tuple-element.38), channel_id=1, source_target_pairs={{0,28},{2,30},{4,24},{6,26},{8,20},{10,22},{12,16},{14,18},{16,12}... | collective-permute-start | bytes 393224 | tf_op jit(solution)/shard_map/ppermute | solution.py:519
  65.1 25.3 %collective-permute-start.11 = (bf16[4,32,1024]{2,1,0:T(8,128)(2,1)S(1)}, bf16[4,32,1024]{2,1,0:T(8,128)(2,1)S(1)}, u32[]{:S(2)}, u32[]{:S(2)}) collective-permute-start(bf16[4,32,1024]{2,1,0:T(8,128)(2,1)S(1)} %constant_dynamic-update-slice_fusion.2.rest_2_), channel_id=1, source_target_pairs={{0,1},{2,3},{4,5},{6,7},{8,9},{10,11},{12,13},{14,15},{16,17},{18,... | collective-permute-start | bytes 786440 | tf_op jit(solution)/shard_map/ppermute | solution.py:465
  68.6 21.8 %collective-permute-start.9 = (bf16[4,32,1024]{2,1,0:T(8,128)(2,1)S(1)}, bf16[4,32,1024]{2,1,0:T(8,128)(2,1)S(1)}, u32[]{:S(2)}, u32[]{:S(2)}) collective-permute-start(bf16[4,32,1024]{2,1,0:T(8,128)(2,1)S(1)} %pad_maximum_fusion.rest_0_), channel_id=1, source_target_pairs={{0,1},{2,3},{4,5},{6,7},{8,9},{10,11},{12,13},{14,15},{16,17},{18,... | collective-permute-start | bytes 786440 | tf_op jit(solution)/shard_map/ppermute | solution.py:465
  74.9 15.5 %collective-permute-start.10 = (bf16[4,32,1024]{2,1,0:T(8,128)(2,1)S(1)}, bf16[4,32,1024]{2,1,0:T(8,128)(2,1)S(1)}, u32[]{:S(2)}, u32[]{:S(2)}) collective-permute-start(bf16[4,32,1024]{2,1,0:T(8,128)(2,1)S(1)} %constant_dynamic-update-slice_fusion.rest_1_), channel_id=1, source_target_pairs={{0,1},{2,3},{4,5},{6,7},{8,9},{10,11},{12,13},{14,15},{16,17},{18,... | collective-permute-start | bytes 786440 | tf_op jit(solution)/shard_map/ppermute | solution.py:465
  78.4 10.6 %collective-permute-start.12 = (bf16[2,32,1024]{2,1,0:T(8,128)(2,1)S(1)}, bf16[2,32,1024]{2,1,0:T(8,128)(2,1)}, u32[]{:S(2)}, u32[]{:S(2)}) collective-permute-start(bf16[2,32,1024]{2,1,0:T(8,128)(2,1)S(1)} %collective-permute-done.7.rest_3_), channel_id=1, source_target_pairs={{0,1},{2,3},{4,5},{6,7},{8,9},{10,11},{12,13},{14,15},{16,17},{18,... | collective-permute-start | bytes 393224 | tf_op jit(solution)/shard_map/ppermute | solution.py:465
  80.3 10.1 %collective-permute-start.13 = (bf16[2,32,1024]{2,1,0:T(8,128)(2,1)S(1)}, bf16[2,32,1024]{2,1,0:T(8,128)(2,1)}, u32[]{:S(2)}, u32[]{:S(2)}) collective-permute-start(bf16[2,32,1024]{2,1,0:T(8,128)(2,1)S(1)} %collective-permute-done.8.rest_4_), channel_id=1, source_target_pairs={{0,1},{2,3},{4,5},{6,7},{8,9},{10,11},{12,13},{14,15},{16,17},{18,... | collective-permute-start | bytes 393224 | tf_op jit(solution)/shard_map/ppermute | solution.py:465

commit v2 on v1

--- a/solution.py
+++ b/solution.py
@@ -11,6 +11,9 @@
 
 RADIX = 128
 STRIPES = 8
+HALVES = 4
+KSTEP = 256
+KTILE = 512
 SPACES = pltpu.MemorySpace
 
 f32 = jnp.float32
@@ -95,78 +98,86 @@
     return slice(at * width, (at + 1) * width)
 
 
-def inverse_kernel(
-    modes,
-    devices,
-    factor,
-    launch,
-    phase,
-    twist,
-    fh,
-    fl,
-    sh,
-    sl,
-    out,
-    natural,
-    turned,
-    launched,
-    phases,
-    sems,
-):
+def inverse_kernel(modes, devices, factor, launch, phase, *rest):
+    tables_in, out, natural, turned, launched, phases = rest[:5], *rest[5:10]
+    tables_here, sems, table_sems = rest[10:15], rest[15], rest[16]
     radix = RADIX
     length = launch.shape[-1]
+    half = modes // 2
     copies = []
-    for at in range(STRIPES):
-        cut = stripe(at, length)
-        copies.append(
-            [
-                pltpu.make_async_copy(
-                    launch.at[:, :, cut], launched.at[:, :, cut], sems.at[2 * at]
-                ),
-                pltpu.make_async_copy(phase.at[:, cut], phases.at[:, cut], sems.at[2 * at + 1]),
+    for side in range(2):
+        rows = slice(side * half, (side + 1) * half)
+        for at in range(HALVES):
+            width = length // HALVES
+            cut = slice(at * width, (at + 1) * width)
+            sem = 2 * (side * HALVES + at)
+            copies.append(
+                [
+                    pltpu.make_async_copy(
+                        launch.at[:, rows, cut], launched.at[:, rows, cut], sems.at[sem]
+                    ),
+                    pltpu.make_async_copy(
+                        phase.at[rows, cut], phases.at[rows, cut], sems.at[sem + 1]
+                    ),
+                ]
+            )
+            for copy in copies[-1]:
+                copy.start()
+        if side == 0:
+            more = [
+                pltpu.make_async_copy(there, here, table_sems.at[at])
+                for at, (there, here) in enumerate(zip(tables_in, tables_here))
             ]
-        )
-        for copy in copies[-1]:
-            copy.start()
-
-    def rotate(k1, carry):
-        at = pl.ds(pl.multiple_of(k1 * radix, radix), radix)
-        rows = pl.ds(pl.multiple_of(k1 * modes, modes), modes)
-        sine, cosine = sincos(phases[:, at] * factor[0, 0])
-        real, imag = launched[0, :, at], launched[1, :, at]
-        natural[0, rows, :] = real * cosine - imag * sine
-        natural[1, rows, :] = real * sine + imag * cosine
-        return carry
-
-    for at in range(STRIPES):
-        for copy in copies[at]:
-            copy.wait()
-        part = radix // STRIPES
-        lax.fori_loop(at * part, (at + 1) * part, rotate, 0, unroll=4)
-    for pair in range(modes // 2):
-        both = []
-        for m in (2 * pair, 2 * pair + 1):
-            both.append(
-                jnp.concatenate([natural[c, pl.ds(m, radix, stride=modes), :] for c in range(2)], 0)
-            )
-        high, low = split(jnp.concatenate(both, 1))
-        section = dot(fh[...], high) + (dot(fh[...], low) + dot(fl[...], high))
-        rows = []
-        for side in range(2):
-            real = section[:radix, side * radix : (side + 1) * radix]
-            imag = section[radix:, side * radix : (side + 1) * radix]
-            rows.append(
-                jnp.concatenate(
-                    [real * twist[0] - imag * twist[1], real * twist[1] + imag * twist[0]], 1
+            for copy in more:
+                copy.start()
+    twist, fh, fl, sh, sl = tables_here
+    for side in range(2):
+
+        def rotate(k1, carry, side=side):
+            at = pl.ds(pl.multiple_of(k1 * radix, radix), radix)
+            rows = pl.ds(pl.multiple_of(k1 * half, half), half)
+            mine = slice(side * half, (side + 1) * half)
+            sine, cosine = sincos(phases[mine, at] * factor[0, 0])
+            real, imag = launched[0, mine, at], launched[1, mine, at]
+            natural[0, rows, :] = real * cosine - imag * sine
+            natural[1, rows, :] = real * sine + imag * cosine
+            return carry
+
+        for at in range(HALVES):
+            for copy in copies[side * HALVES + at]:
+                copy.wait()
+            part = radix // HALVES
+            lax.fori_loop(at * part, (at + 1) * part, rotate, 0, unroll=8)
+        if side == 0:
+            for copy in more:
+                copy.wait()
+        for pair in range(half // 2):
+            both = []
+            for m in (2 * pair, 2 * pair + 1):
+                both.append(
+                    jnp.concatenate(
+                        [natural[c, pl.ds(m, radix, stride=half), :] for c in range(2)], 0
+                    )
                 )
-            )
-        high, low = split(jnp.concatenate(rows, 0))
-        final = dot(high, sh[...]) + (dot(low, sh[...]) + dot(high, sl[...]))
-        for side in range(2):
-            for c in range(2):
-                turned[c, pl.ds(2 * pair + side, radix, stride=modes), :] = final[
-                    side * radix : (side + 1) * radix, c * radix : (c + 1) * radix
-                ]
+            high, low = split(jnp.concatenate(both, 1))
+            section = dot(fh[...], high) + (dot(fh[...], low) + dot(fl[...], high))
+            rows = []
+            for one in range(2):
+                real = section[:radix, one * radix : (one + 1) * radix]
+                imag = section[radix:, one * radix : (one + 1) * radix]
+                rows.append(
+                    jnp.concatenate(
+                        [real * twist[0] - imag * twist[1], real * twist[1] + imag * twist[0]], 1
+                    )
+                )
+            high, low = split(jnp.concatenate(rows, 0))
+            final = dot(high, sh[...]) + (dot(low, sh[...]) + dot(high, sl[...]))
+            for one in range(2):
+                m = side * half + 2 * pair + one
+                for c in range(2):
+                    turned[c, pl.ds(m, radix, stride=modes), :] = final[
+                        one * radix : (one + 1) * radix, c * radix : (c + 1) * radix
+                    ]
     each = radix // devices
     for t2 in range(radix):
         target, slot = divmod(t2, each)
@@ -179,17 +190,20 @@
 def inverse(factor, launch, phase, devices):
     _, modes, length = launch.shape
     table = tables(length)
+    held = [table["twist"], *table["inv_first"], *table["inv_second"]]
     return pl.pallas_call(
         functools.partial(inverse_kernel, modes, devices),
         out_shape=jax.ShapeDtypeStruct((devices, 2 * modes, length // devices), bf16),
-        in_specs=specs("shhvvvvv"),
+        in_specs=specs("shhhhhhh"),
         out_specs=specs("v")[0],
         scratch_shapes=[
-            pltpu.VMEM((2, RADIX * modes, RADIX), f32),
+            pltpu.VMEM((2, RADIX * modes // 2, RADIX), f32),
             pltpu.VMEM((2, RADIX * modes, RADIX), f32),
             pltpu.VMEM(launch.shape, f32),
             pltpu.VMEM(phase.shape, f32),
-            pltpu.SemaphoreType.DMA((2 * STRIPES,)),
+            *[pltpu.VMEM(value.shape, value.dtype) for value in held],
+            pltpu.SemaphoreType.DMA((4 * HALVES,)),
+            pltpu.SemaphoreType.DMA((len(held),)),
         ],
         compiler_params=params(),
         name="inverse",
@@ -197,29 +211,18 @@
         factor,
         *[
             pltpu.with_memory_space_constraint(value, SPACES.HBM)
-            for value in (
-                launch,
-                phase,
-                *map(jnp.asarray, (table["twist"], *table["inv_first"], *table["inv_second"])),
-            )
+            for value in (launch, phase, *map(jnp.asarray, held))
         ],
     )
 
 
-def kerr_kernel(modes, devices, step, me, fields, profiles, flipped, weights, *rest):
+def kerr_kernel(modes, devices, step, lanes, me, fields, profiles, flipped, weights, *rest):
     chips = devices // 2
-    keeps, gives, (gathered, total, spread, sems) = (
-        rest[:chips],
-        rest[chips : chips + 2],
-        rest[-4:],
-    )
-    points = profiles.shape[0]
+    keeps, gives = rest[:chips], rest[chips : chips + 2]
+    gathered, fields_t, total_t, total, sems = rest[chips + 2 :]
+    points, _ = profiles.shape
     width = fields.shape[-1]
-    tiles = 4
-    for at in range(points // RADIX):
-        column = jnp.broadcast_to(weights[at : at + 1, :], (RADIX, RADIX)).T
-        spread[at * RADIX : (at + 1) * RADIX, :] = column
-    lanes = width // tiles
+    tiles = width // lanes
     copies = []
     for tile in range(tiles):
         cut = slice(tile * lanes, (tile + 1) * lanes)
@@ -237,18 +240,28 @@
         cut = slice(tile * lanes, (tile + 1) * lanes)
         for copy in copies[tile * 2 * devices : (tile + 1) * 2 * devices]:
             copy.wait()
-        for at in range(0, points, step):
-            lines = profiles[at : at + step, :]
-            real = dot(lines, gathered[0, :, cut])
-            imag = dot(lines, gathered[1, :, cut])
-            power = jnp.concatenate([spread[at : at + step, :]] * (lanes // RADIX), 1) * (real * real + imag * imag)
-            back = flipped[:, at : at + step]
-            parts = [dot(back, (power * real).astype(bf16)), dot(back, (power * imag).astype(bf16))]
+        for c in range(2):
+            fields_t[c, cut, :] = gathered[c, :, cut].T
+    for at in range(0, points, step):
+        these = slice(at, at + step)
+        for tile in range(tiles):
+            cut = slice(tile * lanes, (tile + 1) * lanes)
+            real = dot(fields_t[0, cut, :], flipped[:, these])
+            imag = dot(fields_t[1, cut, :], flipped[:, these])
+            power = weights[:, these] * (real * real + imag * imag)
+            parts = [
+                dot((power * real).astype(bf16), profiles[these, :]),
+                dot((power * imag).astype(bf16), profiles[these, :]),
+            ]
             if at == 0:
-                total[0, :, cut], total[1, :, cut] = parts
+                total_t[0, cut, :], total_t[1, cut, :] = parts
             else:
-                total[0, :, cut] += parts[0]
-                total[1, :, cut] += parts[1]
+                total_t[0, cut, :] += parts[0]
+                total_t[1, cut, :] += parts[1]
+    for c in range(2):
+        for tile in range(width // RADIX):
+            cut = slice(tile * RADIX, (tile + 1) * RADIX)
+            total[c, :, cut] = total_t[c, cut, :].T
     for hop in range(devices):
         rows = pl.ds(pl.multiple_of((me[0, 0] ^ hop) * modes, modes), modes)
         chip, other = divmod(hop, 2)
@@ -261,16 +274,17 @@
     devices, _, width = fields.shape
     chips = devices // 2
     return pl.pallas_call(
-        functools.partial(kerr_kernel, modes, devices, 1024),
+        functools.partial(kerr_kernel, modes, devices, KSTEP, KTILE),
         out_shape=[jax.ShapeDtypeStruct((2 * modes, width), bf16)] * chips
         + [jax.ShapeDtypeStruct((chips // 2, 2 * modes, width), bf16)] * 2,
         in_specs=specs("savvv"),
         out_specs=specs("v" * (chips + 2)),
         scratch_shapes=[
             pltpu.VMEM((2, devices * modes, width), bf16),
+            pltpu.VMEM((2, width, devices * modes), bf16),
+            pltpu.VMEM((2, width, devices * modes), f32),
             pltpu.VMEM((2, devices * modes, width), f32),
-            pltpu.VMEM((profiles.shape[0], RADIX), f32),
-            pltpu.SemaphoreType.DMA((8 * devices,)),
+            pltpu.SemaphoreType.DMA((2 * devices * (width // KTILE),)),
         ],
         compiler_params=params(),
         name="kerr",
@@ -316,10 +330,14 @@
         write(1, slot, imag * cosine - real * sine)
 
 
-def late_kernel(modes, devices, last, me, factor, base, phase, twist, fh, fl, sh, sl, *rest):
+def late_kernel(modes, devices, first, alone, last, me, factor, base, phase, *rest):
+    (twist, fh, fl, sh, sl), rest = rest[:5], rest[5:]
     count = len(groups_of(devices))
-    groups, out, (turned, final) = rest[:count], rest[count], rest[count + 1 : count + 3]
-    spare = rest[count + 3 :]
+    groups, out, rest = rest[:count], rest[count], rest[count + 1 :]
+    if not alone:
+        ahead, rest = rest[0], rest[1:]
+    turned, final = rest[:2]
+    spare = rest[2:]
     radix = RADIX
     each = radix // devices
     size = each * modes
@@ -351,7 +369,12 @@
     def finish(k1, carry):
         at = pl.ds(pl.multiple_of(k1 * radix, radix), radix)
         rows = pl.ds(pl.multiple_of(k1 * modes, modes), modes)
-        sine, cosine = sincos(phase[:, at] * factor[0, 0])
+        if first:
+            sine, cosine = sincos(phase[:, at] * factor[0, 0])
+        else:
+            sine, cosine = phase[0, :, at], phase[1, :, at]
+        if not alone:
+            ahead[0, :, at], ahead[1, :, at] = sincos(phase[:, at] * (factor[0, 0] - 1.0))
         real, imag = final[0, rows, :], final[1, rows, :]
         result[0, :, at] = base[0, :, at] + (real * cosine + imag * sine)
         result[1, :, at] = base[1, :, at] + (imag * cosine - real * sine)
@@ -371,15 +394,16 @@
         copy.wait()
 
 
-def late(me, factor, groups, base, phase, devices, last):
+def late(me, factor, groups, base, phase, devices, first, last):
     _, modes, length = base.shape
+    ahead = first and not last
     table = tables(length)
     spare = [pltpu.VMEM(base.shape, f32), pltpu.SemaphoreType.DMA((STRIPES,))]
     return pl.pallas_call(
-        functools.partial(late_kernel, modes, devices, last),
-        out_shape=jax.ShapeDtypeStruct(base.shape, f32),
+        functools.partial(late_kernel, modes, devices, first, not ahead, last),
+        out_shape=[jax.ShapeDtypeStruct(base.shape, f32)] * (2 if ahead else 1),
         in_specs=specs("ssvvvvvvv" + "v" * len(groups)),
-        out_specs=specs("h" if last else "v")[0],
+        out_specs=specs("vv" if ahead else "h" if last else "v"),
         scratch_shapes=[pltpu.VMEM((2, RADIX * modes, RADIX), f32)] * 2 + (spare if last else []),
         compiler_params=params(),
         name="late",
@@ -506,7 +530,7 @@
     here = scalar(me, jnp.int32)
     fields = inverse(scalar(place + 1), launch, phase, devices)
     fields = lax.all_to_all(fields, "modes", 0, 0, tiled=True)
-    sent = kerr(here, fields, profiles, profiles.T, weights.reshape(-1, RADIX), modes)
+    sent = kerr(here, fields, profiles, profiles.T, weights[None, :], modes)
     chips = devices // 2
     keeps, (near, far) = sent[:chips], sent[chips:]
     swap = [(a, a ^ 1) for a in range(devices)]
@@ -523,15 +547,19 @@
         waiting.append([pieces] + onward(pieces, points))
     result = launch
     for shift in range(points):
-        result = late(
+        last = shift == points - 1
+        result, *ahead = late(
             here,
             scalar(place + 1 - shift),
             [held[shift] for held in waiting],
             result,
-            phase,
+            turn if shift == 1 else phase,
             devices,
-            shift == points - 1,
+            shift != 1,
+            last,
         )
+        if ahead:
+            turn = ahead[0]
     return result[None]
 
 

time: 97 us -> 94.7 us (0.976)
  local copies, waits for them, and re-layouts: 0.74 us -> 2.33 us
  waiting for transfers between devices: 32.6 us -> 31.1 us
  Pallas kernels: 28 us -> 26.6 us
  starting transfers between devices: 34.9 us -> 33.8 us
    unnamed x19 -> x21, local copies, waits for them, and re-layouts: 0.72 us -> 2.3 us
    ppermute x5, waiting for transfers between devices: 2.12 us -> 0.63 us  [onward(): held.append(lax.ppermute(values, 'gz', pairs))]
    ppermute x5, starting transfers between devices: 12.1 us -> 11 us  [onward(): held.append(lax.ppermute(values, 'gz', pairs))]
  transfers between devices with their start and end apart: 15 -> 15, of which waited for: 6 -> 5; matrix products, arithmetic and copies ran while one was open for 1% -> 1% of each run, Pallas kernels for 6% -> 9%
where the time goes in v2:
time: 94.7 us; the launch traced here: 94.3 us
  starting transfers between devices  33.8 us (36%)
  waiting for transfers between devices  31.1 us (33%)
  Pallas kernels  26.6 us (28%)
  local copies, waits for them, and re-layouts  2.33 us (2%)
    all_to_all x1, waiting for transfers between devices, on_device(): fields = lax.all_to_all(fields, 'modes', 0, 0, tiled=True)  22.2 us
    ppermute x7, starting transfers between devices, on_device(): got[chip] = lax.ppermute(got[chip], 'modes', pairs)  14.4 us
    pallas_call x2, Pallas kernels, late(): pl.pallas_call(functools.partial(late_kernel, modes, devices, first, not...  12.7 us
    ppermute x5, starting transfers between devices, onward(): held.append(lax.ppermute(values, 'gz', pairs))  11 us
    all_to_all x1, starting transfers between devices, on_device(): fields = lax.all_to_all(fields, 'modes', 0, 0, tiled=True)  7.53 us
    pallas_call x1, Pallas kernels, inverse(): pl.pallas_call(functools.partial(inverse_kernel, modes, devices), out_sha...  7.32 us
    ppermute x7, waiting for transfers between devices, on_device(): got[chip] = lax.ppermute(got[chip], 'modes', pairs)  7.2 us
    pallas_call x1, Pallas kernels, kerr(): pl.pallas_call(functools.partial(kerr_kernel, modes, devices, KSTEP, KTIL...  6.48 us
  transfers between devices with their start and end apart: 15, of which 5 were waited for; matrix products, arithmetic and copies ran while one was open for 1% of the time, Pallas kernels for 9%

profile of v2, /device:TPU:0, one launch (start us, length us, event | category | flops | bytes accessed | tf_op | source)
XLA Modules:
  0.0 94.3 jit_solution(4600923344800839128)
XLA Ops:
  0.0 7.3 %inverse.1 = bf16[16,32,1024]{2,1,0:T(8,128)(2,1)} custom-call(f32[1,1]{1,0:T(1,128)} %bitcast.2.factor, f32[2,16,16384]{2,1,0:T(8,128)} %base.1, f32[16,16384]{1,0:T(8,128)} %phase.3, f32[2,128,128]{2,1,0:T(8,128)} %constant.26.clone.rest_0_, bf16[256,256]{1,0:T(8,128)(2,1)} %constant.27.clone.rest_1_, bf16[256,256]{1,0:T(8,128)(2,1)} %constant.28.clone.rest_2_, ...), custom_call_target="tpu_custom_call" | custom-call | tf_op jit(solution)/shard_map/inverse/pallas_call | solution.py:194
  7.3 0.0 copy-start
  7.3 0.0 copy-start.8
  7.3 7.5 %all-to-all-start = ((bf16[16,32,1024]{2,1,0:T(8,128)(2,1)}), bf16[16,32,1024]{2,1,0:T(8,128)(2,1)S(1)}, u32[]{:S(2)}, u32[]{:S(2)}) async-start(bf16[16,32,1024]{2,1,0:T(8,128)(2,1)} %inverse.1), calls=%async_computation | async-start | bytes 2097152 | tf_op jit(solution)/shard_map/all_to_all | solution.py:532
  14.9 0.6 copy.14
  15.6 22.2 %all-to-all-done.fields = bf16[16,32,1024]{2,1,0:T(8,128)(2,1)S(1)} async-done(((bf16[16,32,1024]{2,1,0:T(8,128)(2,1)}), bf16[16,32,1024]{2,1,0:T(8,128)(2,1)S(1)}, u32[]{:S(2)}, u32[]{:S(2)}) %all-to-all-start) | async-done | bytes 1048608 | tf_op jit(solution)/shard_map/all_to_all | solution.py:532
  37.8 6.5 %kerr.1 = (bf16[32,1024]{1,0:T(8,128)(2,1)S(1)}, bf16[32,1024]{1,0:T(8,128)(2,1)S(1)}, bf16[32,1024]{1,0:T(8,128)(2,1)S(1)}, bf16[32,1024]{1,0:T(8,128)(2,1)S(1)...) custom-call(s32[1,1]{1,0:T(1,128)} %bitcast.me, ...), custom_call_target="tpu_custom_call" | custom-call | tf_op jit(solution)/shard_map/kerr/pallas_call | solution.py:276
  44.3 0.0 copy-start.1
  44.3 0.0 copy-start.3
  44.3 0.0 copy-start.4
  44.3 0.0 copy-start.5
  44.3 0.0 copy-start.6
  44.3 0.0 copy-start.7
  44.3 0.8 collective-permute-start
  45.1 0.1 collective-permute-start.2
  45.2 1.1 %collective-permute-done.refs_3_ = bf16[4,32,1024]{2,1,0:T(8,128)(2,1)S(1)} collective-permute-done((bf16[4,32,1024]{2,1,0:T(8,128)(2,1)S(1)}, bf16[4,32,1024]{2,1,0:T(8,128)(2,1)S(1)}, u32[]{:S(2)}, u32[]{:S(2)}) %collective-permute-start) | collective-permute-done | bytes 262176 | tf_op jit(solution)/shard_map/ppermute | solution.py:538
  46.3 3.4 %collective-permute-start.5 = (bf16[2,32,1024]{2,1,0:T(8,128)(2,1)S(1)}, bf16[2,32,1024]{2,1,0:T(8,128)(2,1)S(1)}, u32[]{:S(2)}, u32[]{:S(2)}) collective-permute-start(bf16[2,32,1024]{2,1,0:T(8,128)(2,1)S(1)} %get-tuple-element.37), channel_id=1, source_target_pairs={{0,8},{2,10},{4,12},{6,14},{8,0},{10,2},{12,4},{14,6},{16,24},{18,... | collective-permute-start | bytes 393224 | tf_op jit(solution)/shard_map/ppermute | solution.py:543
  49.7 0.9 collective-permute-start.6
  50.7 0.6 collective-permute-start.1
  51.3 0.0 collective-permute-done.2.refs_4_
  51.3 3.4 %collective-permute-start.3 = (bf16[2,32,1024]{2,1,0:T(8,128)(2,1)S(1)}, bf16[2,32,1024]{2,1,0:T(8,128)(2,1)S(1)}, u32[]{:S(2)}, u32[]{:S(2)}) collective-permute-start(bf16[2,32,1024]{2,1,0:T(8,128)(2,1)S(1)} %get-tuple-element.35), channel_id=1, source_target_pairs={{0,16},{2,18},{4,20},{6,22},{8,24},{10,26},{12,28},{14,30},{16,0},... | collective-permute-start | bytes 393224 | tf_op jit(solution)/shard_map/ppermute | solution.py:543
  54.7 0.4 collective-permute-start.4
  55.2 0.0 collective-permute-done.5
  55.2 2.9 %collective-permute-start.7 = (bf16[2,32,1024]{2,1,0:T(8,128)(2,1)S(1)}, bf16[2,32,1024]{2,1,0:T(8,128)(2,1)}, u32[]{:S(2)}, u32[]{:S(2)}) collective-permute-start(bf16[2,32,1024]{2,1,0:T(8,128)(2,1)S(1)} %get-tuple-element.39), channel_id=1, source_target_pairs={{0,24},{2,26},{4,28},{6,30},{8,16},{10,18},{12,20},{14,22},{16,8},... | collective-permute-start | bytes 393224 | tf_op jit(solution)/shard_map/ppermute | solution.py:543
  58.1 2.2 %collective-permute-done.6 = bf16[2,32,1024]{2,1,0:T(8,128)(2,1)S(1)} collective-permute-done((bf16[2,32,1024]{2,1,0:T(8,128)(2,1)S(1)}, bf16[2,32,1024]{2,1,0:T(8,128)(2,1)S(1)}, u32[]{:S(2)}, u32[]{:S(2)}) %collective-permute-start.6) | collective-permute-done | bytes 131104 | tf_op jit(solution)/shard_map/ppermute | solution.py:543
  60.3 2.7 %collective-permute-start.8 = (bf16[2,32,1024]{2,1,0:T(8,128)(2,1)S(1)}, bf16[2,32,1024]{2,1,0:T(8,128)(2,1)}, u32[]{:S(2)}, u32[]{:S(2)}) collective-permute-start(bf16[2,32,1024]{2,1,0:T(8,128)(2,1)S(1)} %get-tuple-element.40), channel_id=1, source_target_pairs={{0,28},{2,30},{4,24},{6,26},{8,20},{10,22},{12,16},{14,18},{16,12}... | collective-permute-start | bytes 393224 | tf_op jit(solution)/shard_map/ppermute | solution.py:543
  63.0 0.0 collective-permute-done.1
  63.0 3.4 %collective-permute-start.11 = (bf16[4,32,1024]{2,1,0:T(8,128)(2,1)S(1)}, bf16[4,32,1024]{2,1,0:T(8,128)(2,1)S(1)}, u32[]{:S(2)}, u32[]{:S(2)}) collective-permute-start(bf16[4,32,1024]{2,1,0:T(8,128)(2,1)S(1)} %constant_dynamic-update-slice_fusion.2.rest_7_), channel_id=1, source_target_pairs={{0,1},{2,3},{4,5},{6,7},{8,9},{10,11},{12,13},{14,15},{16,17},{18,... | collective-permute-start | bytes 786440 | tf_op jit(solution)/shard_map/ppermute | solution.py:489
  66.5 0.0 collective-permute-done.3
  66.5 1.3 %collective-permute-start.9 = (bf16[4,32,1024]{2,1,0:T(8,128)(2,1)S(1)}, bf16[4,32,1024]{2,1,0:T(8,128)(2,1)S(1)}, u32[]{:S(2)}, u32[]{:S(2)}) collective-permute-start(bf16[4,32,1024]{2,1,0:T(8,128)(2,1)S(1)} %pad_maximum_fusion.rest_5_), channel_id=1, source_target_pairs={{0,1},{2,3},{4,5},{6,7},{8,9},{10,11},{12,13},{14,15},{16,17},{18,... | collective-permute-start | bytes 786440 | tf_op jit(solution)/shard_map/ppermute | solution.py:489
  67.9 5.0 %collective-permute-done.4 = bf16[2,32,1024]{2,1,0:T(8,128)(2,1)S(1)} collective-permute-done((bf16[2,32,1024]{2,1,0:T(8,128)(2,1)S(1)}, bf16[2,32,1024]{2,1,0:T(8,128)(2,1)S(1)}, u32[]{:S(2)}, u32[]{:S(2)}) %collective-permute-start.4) | collective-permute-done | bytes 131104 | tf_op jit(solution)/shard_map/ppermute | solution.py:543
  72.9 3.4 %collective-permute-start.10 = (bf16[4,32,1024]{2,1,0:T(8,128)(2,1)S(1)}, bf16[4,32,1024]{2,1,0:T(8,128)(2,1)S(1)}, u32[]{:S(2)}, u32[]{:S(2)}) collective-permute-start(bf16[4,32,1024]{2,1,0:T(8,128)(2,1)S(1)} %constant_dynamic-update-slice_fusion.rest_6_), channel_id=1, source_target_pairs={{0,1},{2,3},{4,5},{6,7},{8,9},{10,11},{12,13},{14,15},{16,17},{18,... | collective-permute-start | bytes 786440 | tf_op jit(solution)/shard_map/ppermute | solution.py:489
  76.3 0.0 collective-permute-done.7.rest_8_
  76.3 1.3 %collective-permute-start.12 = (bf16[2,32,1024]{2,1,0:T(8,128)(2,1)}, bf16[2,32,1024]{2,1,0:T(8,128)(2,1)S(1)}, u32[]{:S(2)}, u32[]{:S(2)}) collective-permute-start(bf16[2,32,1024]{2,1,0:T(8,128)(2,1)} %collective-permute-done.7.rest_8_), channel_id=1, source_target_pairs={{0,1},{2,3},{4,5},{6,7},{8,9},{10,11},{12,13},{14,15},{16,17},{18,... | collective-permute-start | bytes 393224 | tf_op jit(solution)/shard_map/ppermute | solution.py:489
  77.6 0.0 collective-permute-done.8.rest_9_
  77.6 1.5 %collective-permute-start.13 = (bf16[2,32,1024]{2,1,0:T(8,128)(2,1)}, bf16[2,32,1024]{2,1,0:T(8,128)(2,1)S(1)}, u32[]{:S(2)}, u32[]{:S(2)}) collective-permute-start(bf16[2,32,1024]{2,1,0:T(8,128)(2,1)} %collective-permute-done.8.rest_9_), channel_id=1, source_target_pairs={{0,1},{2,3},{4,5},{6,7},{8,9},{10,11},{12,13},{14,15},{16,17},{18,... | collective-permute-start | bytes 393224 | tf_op jit(solution)/shard_map/ppermute | solution.py:489
  79.1 0.0 copy-done.1
  79.1 0.0 copy-done.3
  79.1 0.0 copy-done.4
  79.2 8.6 %late.2 = (f32[2,16,16384]{2,1,0:T(8,128)S(1)}, f32[2,16,16384]{2,1,0:T(8,128)}) custom-call(s32[1,1]{1,0:T(1,128)} %bitcast.me, f32[1,1]{1,0:T(1,128)} %bitcast.2.factor, f32[2,16,16384]{2,1,0:T(8,128)} %base.1, f32[16,16384]{1,0:T(8,128)S(1)} %copy-done.1, f32[2,128,128]{2,1,0:T(8,128)S(1)} %copy-done.5, bf16[256,256]{1,0:T(8,128)(2,1)S(1)} %copy-done.7, ...), custom_call_target="tpu_custom_call" | custom-call | tf_op jit(solution)/shard_map/late/pallas_call | solution.py:402
  87.8 0.0 collective-permute-done.12.rest_8_
  87.8 0.6 collective-permute-done.13.rest_9_
  88.4 0.0 collective-permute-done.11.rest_7_
  88.4 0.0 collective-permute-done.9.rest_5_
  88.4 0.0 collective-permute-done.10.rest_6_
  88.4 0.0 copy-start.2
  88.5 1.6 %copy-done.2 = f32[2,16,16384]{2,1,0:T(8,128)S(1)} copy-done((f32[2,16,16384]{2,1,0:T(8,128)S(1)}, f32[2,16,16384]{2,1,0:T(8,128)}, u32[]{:S(2)}) %copy-start.2) | copy-done | bytes 2097176
  90.0 4.1 %late.3 = f32[2,16,16384]{2,1,0:T(8,128)} custom-call(s32[1,1]{1,0:T(1,128)} %bitcast.me, f32[1,1]{1,0:T(1,128)} %bitcast.1.factor, f32[2,16,16384]{2,1,0:T(8,128)S(1)} %get-tuple-element.41.base, f32[2,16,16384]{2,1,0:T(8,128)S(1)} %copy-done.2, f32[2,128,128]{2,1,0:T(8,128)S(1)} %copy-done.5, bf16[256,256]{1,0:T(8,128)(2,1)S(1)} %copy-done.7, ...), custom_call_target="tpu_custom_call" | custom-call | tf_op jit(solution)/shard_map/late/pallas_call | solution.py:402
  (13 shorter events, 0.1 us)
Async XLA Ops:
  7.3 7.6 %copy-start = (bf16[2048,256]{1,0:T(8,128)(2,1)S(1)}, bf16[2048,256]{1,0:T(8,128)(2,1)}, u32[]{:S(2)}) copy-start(bf16[2048,256]{1,0:T(8,128)(2,1)} %profiles.1) | copy-start | bytes 3145732
  7.3 30.4 %copy-start.8 = (f32[2048]{0:T(1024)S(1)}, f32[2048]{0:T(1024)}, u32[]{:S(2)}) copy-start(f32[2048]{0:T(1024)} %param.16) | copy-start | bytes 24580
  7.3 30.4 %all-to-all-start = ((bf16[16,32,1024]{2,1,0:T(8,128)(2,1)}), bf16[16,32,1024]{2,1,0:T(8,128)(2,1)S(1)}, u32[]{:S(2)}, u32[]{:S(2)}) async-start(bf16[16,32,1024]{2,1,0:T(8,128)(2,1)} %inverse.1), calls=%async_computation | async-start | bytes 2097152 | tf_op jit(solution)/shard_map/all_to_all | solution.py:532
  44.3 34.8 %copy-start.1 = (f32[16,16384]{1,0:T(8,128)S(1)}, f32[16,16384]{1,0:T(8,128)}, u32[]{:S(2)}) copy-start(f32[16,16384]{1,0:T(8,128)} %phase.3) | copy-start | bytes 3145732
  44.3 34.8 %copy-start.3 = (bf16[256,256]{1,0:T(8,128)(2,1)S(1)}, bf16[256,256]{1,0:T(8,128)(2,1)}, u32[]{:S(2)}) copy-start(bf16[256,256]{1,0:T(8,128)(2,1)} %constant.30.clone.rest_4_) | copy-start | bytes 393220
  44.3 34.8 %copy-start.4 = (bf16[256,256]{1,0:T(8,128)(2,1)S(1)}, bf16[256,256]{1,0:T(8,128)(2,1)}, u32[]{:S(2)}) copy-start(bf16[256,256]{1,0:T(8,128)(2,1)} %constant.29.clone.rest_3_) | copy-start | bytes 393220
  44.3 34.8 %copy-start.5 = (f32[2,128,128]{2,1,0:T(8,128)S(1)}, f32[2,128,128]{2,1,0:T(8,128)}, u32[]{:S(2)}) copy-start(f32[2,128,128]{2,1,0:T(8,128)} %constant.26.clone.rest_0_) | copy-start | bytes 393220
  44.3 34.8 %copy-start.6 = (bf16[256,256]{1,0:T(8,128)(2,1)S(1)}, bf16[256,256]{1,0:T(8,128)(2,1)}, u32[]{:S(2)}) copy-start(bf16[256,256]{1,0:T(8,128)(2,1)} %constant.32.clone.rest_2_) | copy-start | bytes 393220
  44.3 34.8 %copy-start.7 = (bf16[256,256]{1,0:T(8,128)(2,1)S(1)}, bf16[256,256]{1,0:T(8,128)(2,1)}, u32[]{:S(2)}) copy-start(bf16[256,256]{1,0:T(8,128)(2,1)} %constant.31.clone.rest_1_) | copy-start | bytes 393220
  44.3 1.9 %collective-permute-start = (bf16[4,32,1024]{2,1,0:T(8,128)(2,1)S(1)}, bf16[4,32,1024]{2,1,0:T(8,128)(2,1)S(1)}, u32[]{:S(2)}, u32[]{:S(2)}) collective-permute-start(bf16[4,32,1024]{2,1,0:T(8,128)(2,1)S(1)} %get-tuple-element.25), channel_id=1, source_target_pairs={{0,2},{2,0},{4,6},{6,4},{8,10},{10,8},{12,14},{14,12},{16,18},{18,... | collective-permute-start | bytes 786440 | tf_op jit(solution)/shard_map/ppermute | solution.py:538
  45.1 6.2 %collective-permute-start.2 = (bf16[4,32,1024]{2,1,0:T(8,128)(2,1)S(1)}, bf16[4,32,1024]{2,1,0:T(8,128)(2,1)S(1)}, u32[]{:S(2)}, u32[]{:S(2)}) collective-permute-start(bf16[4,32,1024]{2,1,0:T(8,128)(2,1)S(1)} %get-tuple-element.34), channel_id=1, source_target_pairs={{0,2},{2,0},{4,6},{6,4},{8,10},{10,8},{12,14},{14,12},{16,18},{18,... | collective-permute-start | bytes 786440 | tf_op jit(solution)/shard_map/ppermute | solution.py:537
  46.3 8.9 %collective-permute-start.5 = (bf16[2,32,1024]{2,1,0:T(8,128)(2,1)S(1)}, bf16[2,32,1024]{2,1,0:T(8,128)(2,1)S(1)}, u32[]{:S(2)}, u32[]{:S(2)}) collective-permute-start(bf16[2,32,1024]{2,1,0:T(8,128)(2,1)S(1)} %get-tuple-element.37), channel_id=1, source_target_pairs={{0,8},{2,10},{4,12},{6,14},{8,0},{10,2},{12,4},{14,6},{16,24},{18,... | collective-permute-start | bytes 393224 | tf_op jit(solution)/shard_map/ppermute | solution.py:543
  49.7 10.6 %collective-permute-start.6 = (bf16[2,32,1024]{2,1,0:T(8,128)(2,1)S(1)}, bf16[2,32,1024]{2,1,0:T(8,128)(2,1)S(1)}, u32[]{:S(2)}, u32[]{:S(2)}) collective-permute-start(bf16[2,32,1024]{2,1,0:T(8,128)(2,1)S(1)} %get-tuple-element.38), channel_id=1, source_target_pairs={{0,12},{2,14},{4,8},{6,10},{8,4},{10,6},{12,0},{14,2},{16,28},{18,... | collective-permute-start | bytes 393224 | tf_op jit(solution)/shard_map/ppermute | solution.py:543
  50.7 12.4 %collective-permute-start.1 = (bf16[2,32,1024]{2,1,0:T(8,128)(2,1)S(1)}, bf16[2,32,1024]{2,1,0:T(8,128)(2,1)S(1)}, u32[]{:S(2)}, u32[]{:S(2)}) collective-permute-start(bf16[2,32,1024]{2,1,0:T(8,128)(2,1)S(1)} %get-tuple-element.29), channel_id=1, source_target_pairs={{0,4},{2,6},{4,0},{6,2},{8,12},{10,14},{12,8},{14,10},{16,20},{18,... | collective-permute-start | bytes 393224 | tf_op jit(solution)/shard_map/ppermute | solution.py:543
  51.3 15.2 %collective-permute-start.3 = (bf16[2,32,1024]{2,1,0:T(8,128)(2,1)S(1)}, bf16[2,32,1024]{2,1,0:T(8,128)(2,1)S(1)}, u32[]{:S(2)}, u32[]{:S(2)}) collective-permute-start(bf16[2,32,1024]{2,1,0:T(8,128)(2,1)S(1)} %get-tuple-element.35), channel_id=1, source_target_pairs={{0,16},{2,18},{4,20},{6,22},{8,24},{10,26},{12,28},{14,30},{16,0},... | collective-permute-start | bytes 393224 | tf_op jit(solution)/shard_map/ppermute | solution.py:543
  54.7 18.1 %collective-permute-start.4 = (bf16[2,32,1024]{2,1,0:T(8,128)(2,1)S(1)}, bf16[2,32,1024]{2,1,0:T(8,128)(2,1)S(1)}, u32[]{:S(2)}, u32[]{:S(2)}) collective-permute-start(bf16[2,32,1024]{2,1,0:T(8,128)(2,1)S(1)} %get-tuple-element.36), channel_id=1, source_target_pairs={{0,20},{2,22},{4,16},{6,18},{8,28},{10,30},{12,24},{14,26},{16,4},... | collective-permute-start | bytes 393224 | tf_op jit(solution)/shard_map/ppermute | solution.py:543
  55.2 21.1 %collective-permute-start.7 = (bf16[2,32,1024]{2,1,0:T(8,128)(2,1)S(1)}, bf16[2,32,1024]{2,1,0:T(8,128)(2,1)}, u32[]{:S(2)}, u32[]{:S(2)}) collective-permute-start(bf16[2,32,1024]{2,1,0:T(8,128)(2,1)S(1)} %get-tuple-element.39), channel_id=1, source_target_pairs={{0,24},{2,26},{4,28},{6,30},{8,16},{10,18},{12,20},{14,22},{16,8},... | collective-permute-start | bytes 393224 | tf_op jit(solution)/shard_map/ppermute | solution.py:543
  60.3 17.3 %collective-permute-start.8 = (bf16[2,32,1024]{2,1,0:T(8,128)(2,1)S(1)}, bf16[2,32,1024]{2,1,0:T(8,128)(2,1)}, u32[]{:S(2)}, u32[]{:S(2)}) collective-permute-start(bf16[2,32,1024]{2,1,0:T(8,128)(2,1)S(1)} %get-tuple-element.40), channel_id=1, source_target_pairs={{0,28},{2,30},{4,24},{6,26},{8,20},{10,22},{12,16},{14,18},{16,12}... | collective-permute-start | bytes 393224 | tf_op jit(solution)/shard_map/ppermute | solution.py:543
  63.0 25.4 %collective-permute-start.11 = (bf16[4,32,1024]{2,1,0:T(8,128)(2,1)S(1)}, bf16[4,32,1024]{2,1,0:T(8,128)(2,1)S(1)}, u32[]{:S(2)}, u32[]{:S(2)}) collective-permute-start(bf16[4,32,1024]{2,1,0:T(8,128)(2,1)S(1)} %constant_dynamic-update-slice_fusion.2.rest_7_), channel_id=1, source_target_pairs={{0,1},{2,3},{4,5},{6,7},{8,9},{10,11},{12,13},{14,15},{16,17},{18,... | collective-permute-start | bytes 786440 | tf_op jit(solution)/shard_map/ppermute | solution.py:489
  66.5 21.9 %collective-permute-start.9 = (bf16[4,32,1024]{2,1,0:T(8,128)(2,1)S(1)}, bf16[4,32,1024]{2,1,0:T(8,128)(2,1)S(1)}, u32[]{:S(2)}, u32[]{:S(2)}) collective-permute-start(bf16[4,32,1024]{2,1,0:T(8,128)(2,1)S(1)} %pad_maximum_fusion.rest_5_), channel_id=1, source_target_pairs={{0,1},{2,3},{4,5},{6,7},{8,9},{10,11},{12,13},{14,15},{16,17},{18,... | collective-permute-start | bytes 786440 | tf_op jit(solution)/shard_map/ppermute | solution.py:489
  72.9 15.6 %collective-permute-start.10 = (bf16[4,32,1024]{2,1,0:T(8,128)(2,1)S(1)}, bf16[4,32,1024]{2,1,0:T(8,128)(2,1)S(1)}, u32[]{:S(2)}, u32[]{:S(2)}) collective-permute-start(bf16[4,32,1024]{2,1,0:T(8,128)(2,1)S(1)} %constant_dynamic-update-slice_fusion.rest_6_), channel_id=1, source_target_pairs={{0,1},{2,3},{4,5},{6,7},{8,9},{10,11},{12,13},{14,15},{16,17},{18,... | collective-permute-start | bytes 786440 | tf_op jit(solution)/shard_map/ppermute | solution.py:489
  76.3 11.5 %collective-permute-start.12 = (bf16[2,32,1024]{2,1,0:T(8,128)(2,1)}, bf16[2,32,1024]{2,1,0:T(8,128)(2,1)S(1)}, u32[]{:S(2)}, u32[]{:S(2)}) collective-permute-start(bf16[2,32,1024]{2,1,0:T(8,128)(2,1)} %collective-permute-done.7.rest_8_), channel_id=1, source_target_pairs={{0,1},{2,3},{4,5},{6,7},{8,9},{10,11},{12,13},{14,15},{16,17},{18,... | collective-permute-start | bytes 393224 | tf_op jit(solution)/shard_map/ppermute | solution.py:489
  77.6 10.8 %collective-permute-start.13 = (bf16[2,32,1024]{2,1,0:T(8,128)(2,1)}, bf16[2,32,1024]{2,1,0:T(8,128)(2,1)S(1)}, u32[]{:S(2)}, u32[]{:S(2)}) collective-permute-start(bf16[2,32,1024]{2,1,0:T(8,128)(2,1)} %collective-permute-done.8.rest_9_), channel_id=1, source_target_pairs={{0,1},{2,3},{4,5},{6,7},{8,9},{10,11},{12,13},{14,15},{16,17},{18,... | collective-permute-start | bytes 393224 | tf_op jit(solution)/shard_map/ppermute | solution.py:489
  88.4 1.6 %copy-start.2 = (f32[2,16,16384]{2,1,0:T(8,128)S(1)}, f32[2,16,16384]{2,1,0:T(8,128)}, u32[]{:S(2)}) copy-start(f32[2,16,16384]{2,1,0:T(8,128)} %get-tuple-element.42.phase) | copy-start | bytes 6291460

commit v3 on v2

--- a/solution.py
+++ b/solution.py
@@ -338,6 +338,16 @@
         ahead, rest = rest[0], rest[1:]
     turned, final = rest[:2]
     spare = rest[2:]
+    length = base.shape[-1]
+    inward = []
+    if not first:
+        *spare, turns, arrive = spare
+        for at in range(STRIPES):
+            cut = stripe(at, length)
+            inward.append(
+                pltpu.make_async_copy(phase.at[:, :, cut], turns.at[:, :, cut], arrive.at[at])
+            )
+            inward[-1].start()
     radix = RADIX
     each = radix // devices
     size = each * modes
@@ -372,7 +382,7 @@
         if first:
             sine, cosine = sincos(phase[:, at] * factor[0, 0])
         else:
-            sine, cosine = phase[0, :, at], phase[1, :, at]
+            sine, cosine = turns[0, :, at], turns[1, :, at]
         if not alone:
             ahead[0, :, at], ahead[1, :, at] = sincos(phase[:, at] * (factor[0, 0] - 1.0))
         real, imag = final[0, rows, :], final[1, rows, :]
@@ -384,6 +394,8 @@
     for at in range(STRIPES):
         cut = stripe(at, length)
         part = radix // STRIPES
+        if not first:
+            inward[at].wait()
         lax.fori_loop(at * part, (at + 1) * part, finish, 0, unroll=4)
         if last:
             copies.append(
@@ -399,12 +411,15 @@
     ahead = first and not last
     table = tables(length)
     spare = [pltpu.VMEM(base.shape, f32), pltpu.SemaphoreType.DMA((STRIPES,))]
+    spare = spare * last + spare * (not first)
+    if not first:
+        phase = pltpu.with_memory_space_constraint(phase, SPACES.HBM)
     return pl.pallas_call(
         functools.partial(late_kernel, modes, devices, first, not ahead, last),
         out_shape=[jax.ShapeDtypeStruct(base.shape, f32)] * (2 if ahead else 1),
-        in_specs=specs("ssvvvvvvv" + "v" * len(groups)),
+        in_specs=specs("ssv" + ("v" if first else "h") + "vvvvv" + "v" * len(groups)),
         out_specs=specs("vv" if ahead else "h" if last else "v"),
-        scratch_shapes=[pltpu.VMEM((2, RADIX * modes, RADIX), f32)] * 2 + (spare if last else []),
+        scratch_shapes=[pltpu.VMEM((2, RADIX * modes, RADIX), f32)] * 2 + spare,
         compiler_params=params(),
         name="late",
     )(

time: 94.7 us -> 93.8 us (level)
  local copies, waits for them, and re-layouts: 2.33 us -> 0.74 us
    unnamed x21 -> x19, local copies, waits for them, and re-layouts: 2.3 us -> 0.72 us
where the time goes in v3:
time: 93.8 us; the launch traced here: 93.5 us
  starting transfers between devices  33.8 us (36%)
  waiting for transfers between devices  31.1 us (33%)
  Pallas kernels  27.4 us (29%)
    all_to_all x1, waiting for transfers between devices, on_device(): fields = lax.all_to_all(fields, 'modes', 0, 0, tiled=True)  22.2 us
    ppermute x7, starting transfers between devices, on_device(): got[chip] = lax.ppermute(got[chip], 'modes', pairs)  14.4 us
    pallas_call x2, Pallas kernels, late(): pl.pallas_call(functools.partial(late_kernel, modes, devices, first, not...  13.5 us
    ppermute x5, starting transfers between devices, onward(): held.append(lax.ppermute(values, 'gz', pairs))  11 us
    all_to_all x1, starting transfers between devices, on_device(): fields = lax.all_to_all(fields, 'modes', 0, 0, tiled=True)  7.53 us
    pallas_call x1, Pallas kernels, inverse(): pl.pallas_call(functools.partial(inverse_kernel, modes, devices), out_sha...  7.32 us
    ppermute x7, waiting for transfers between devices, on_device(): got[chip] = lax.ppermute(got[chip], 'modes', pairs)  7.2 us
    pallas_call x1, Pallas kernels, kerr(): pl.pallas_call(functools.partial(kerr_kernel, modes, devices, KSTEP, KTIL...  6.48 us
  transfers between devices with their start and end apart: 15, of which 5 were waited for; matrix products, arithmetic and copies ran while one was open for 1% of the time, Pallas kernels for 9%

profile of v3, /device:TPU:0, one launch (start us, length us, event | category | flops | bytes accessed | tf_op | source)
XLA Modules:
  0.0 93.5 jit_solution(606988332107590154)
XLA Ops:
  0.0 7.3 %inverse.1 = bf16[16,32,1024]{2,1,0:T(8,128)(2,1)} custom-call(f32[1,1]{1,0:T(1,128)} %bitcast.2.factor, f32[2,16,16384]{2,1,0:T(8,128)} %base.1, f32[16,16384]{1,0:T(8,128)} %phase.3, f32[2,128,128]{2,1,0:T(8,128)} %constant.26.clone.rest_0_, bf16[256,256]{1,0:T(8,128)(2,1)} %constant.27.clone.rest_1_, bf16[256,256]{1,0:T(8,128)(2,1)} %constant.28.clone.rest_2_, ...), custom_call_target="tpu_custom_call" | custom-call | tf_op jit(solution)/shard_map/inverse/pallas_call | solution.py:194
  7.3 0.0 copy-start
  7.3 0.0 copy-start.7
  7.3 7.5 %all-to-all-start = ((bf16[16,32,1024]{2,1,0:T(8,128)(2,1)}), bf16[16,32,1024]{2,1,0:T(8,128)(2,1)S(1)}, u32[]{:S(2)}, u32[]{:S(2)}) async-start(bf16[16,32,1024]{2,1,0:T(8,128)(2,1)} %inverse.1), calls=%async_computation | async-start | bytes 2097152 | tf_op jit(solution)/shard_map/all_to_all | solution.py:547
  14.9 0.6 copy.14
  15.6 22.2 %all-to-all-done.fields = bf16[16,32,1024]{2,1,0:T(8,128)(2,1)S(1)} async-done(((bf16[16,32,1024]{2,1,0:T(8,128)(2,1)}), bf16[16,32,1024]{2,1,0:T(8,128)(2,1)S(1)}, u32[]{:S(2)}, u32[]{:S(2)}) %all-to-all-start) | async-done | bytes 1048608 | tf_op jit(solution)/shard_map/all_to_all | solution.py:547
  37.8 6.5 %kerr.1 = (bf16[32,1024]{1,0:T(8,128)(2,1)S(1)}, bf16[32,1024]{1,0:T(8,128)(2,1)S(1)}, bf16[32,1024]{1,0:T(8,128)(2,1)S(1)}, bf16[32,1024]{1,0:T(8,128)(2,1)S(1)...) custom-call(s32[1,1]{1,0:T(1,128)} %bitcast.me, ...), custom_call_target="tpu_custom_call" | custom-call | tf_op jit(solution)/shard_map/kerr/pallas_call | solution.py:276
  44.3 0.0 copy-start.1
  44.3 0.0 copy-start.2
  44.3 0.0 copy-start.3
  44.3 0.0 copy-start.4
  44.3 0.0 copy-start.5
  44.3 0.0 copy-start.6
  44.3 0.8 collective-permute-start
  45.1 0.1 collective-permute-start.2
  45.2 1.1 %collective-permute-done.refs_3_ = bf16[4,32,1024]{2,1,0:T(8,128)(2,1)S(1)} collective-permute-done((bf16[4,32,1024]{2,1,0:T(8,128)(2,1)S(1)}, bf16[4,32,1024]{2,1,0:T(8,128)(2,1)S(1)}, u32[]{:S(2)}, u32[]{:S(2)}) %collective-permute-start) | collective-permute-done | bytes 262176 | tf_op jit(solution)/shard_map/ppermute | solution.py:553
  46.3 3.4 %collective-permute-start.5 = (bf16[2,32,1024]{2,1,0:T(8,128)(2,1)S(1)}, bf16[2,32,1024]{2,1,0:T(8,128)(2,1)S(1)}, u32[]{:S(2)}, u32[]{:S(2)}) collective-permute-start(bf16[2,32,1024]{2,1,0:T(8,128)(2,1)S(1)} %get-tuple-element.37), channel_id=1, source_target_pairs={{0,8},{2,10},{4,12},{6,14},{8,0},{10,2},{12,4},{14,6},{16,24},{18,... | collective-permute-start | bytes 393224 | tf_op jit(solution)/shard_map/ppermute | solution.py:558
  49.7 0.9 collective-permute-start.6
  50.7 0.6 collective-permute-start.1
  51.3 0.0 collective-permute-done.2.refs_4_
  51.3 3.4 %collective-permute-start.3 = (bf16[2,32,1024]{2,1,0:T(8,128)(2,1)S(1)}, bf16[2,32,1024]{2,1,0:T(8,128)(2,1)S(1)}, u32[]{:S(2)}, u32[]{:S(2)}) collective-permute-start(bf16[2,32,1024]{2,1,0:T(8,128)(2,1)S(1)} %get-tuple-element.35), channel_id=1, source_target_pairs={{0,16},{2,18},{4,20},{6,22},{8,24},{10,26},{12,28},{14,30},{16,0},... | collective-permute-start | bytes 393224 | tf_op jit(solution)/shard_map/ppermute | solution.py:558
  54.7 0.4 collective-permute-start.4
  55.2 0.0 collective-permute-done.5
  55.2 2.9 %collective-permute-start.7 = (bf16[2,32,1024]{2,1,0:T(8,128)(2,1)S(1)}, bf16[2,32,1024]{2,1,0:T(8,128)(2,1)}, u32[]{:S(2)}, u32[]{:S(2)}) collective-permute-start(bf16[2,32,1024]{2,1,0:T(8,128)(2,1)S(1)} %get-tuple-element.39), channel_id=1, source_target_pairs={{0,24},{2,26},{4,28},{6,30},{8,16},{10,18},{12,20},{14,22},{16,8},... | collective-permute-start | bytes 393224 | tf_op jit(solution)/shard_map/ppermute | solution.py:558
  58.1 2.2 %collective-permute-done.6 = bf16[2,32,1024]{2,1,0:T(8,128)(2,1)S(1)} collective-permute-done((bf16[2,32,1024]{2,1,0:T(8,128)(2,1)S(1)}, bf16[2,32,1024]{2,1,0:T(8,128)(2,1)S(1)}, u32[]{:S(2)}, u32[]{:S(2)}) %collective-permute-start.6) | collective-permute-done | bytes 131104 | tf_op jit(solution)/shard_map/ppermute | solution.py:558
  60.3 2.7 %collective-permute-start.8 = (bf16[2,32,1024]{2,1,0:T(8,128)(2,1)S(1)}, bf16[2,32,1024]{2,1,0:T(8,128)(2,1)}, u32[]{:S(2)}, u32[]{:S(2)}) collective-permute-start(bf16[2,32,1024]{2,1,0:T(8,128)(2,1)S(1)} %get-tuple-element.40), channel_id=1, source_target_pairs={{0,28},{2,30},{4,24},{6,26},{8,20},{10,22},{12,16},{14,18},{16,12}... | collective-permute-start | bytes 393224 | tf_op jit(solution)/shard_map/ppermute | solution.py:558
  63.0 0.0 collective-permute-done.1
  63.0 3.4 %collective-permute-start.11 = (bf16[4,32,1024]{2,1,0:T(8,128)(2,1)S(1)}, bf16[4,32,1024]{2,1,0:T(8,128)(2,1)S(1)}, u32[]{:S(2)}, u32[]{:S(2)}) collective-permute-start(bf16[4,32,1024]{2,1,0:T(8,128)(2,1)S(1)} %constant_dynamic-update-slice_fusion.2.rest_7_), channel_id=1, source_target_pairs={{0,1},{2,3},{4,5},{6,7},{8,9},{10,11},{12,13},{14,15},{16,17},{18,... | collective-permute-start | bytes 786440 | tf_op jit(solution)/shard_map/ppermute | solution.py:504
  66.5 0.0 collective-permute-done.3
  66.5 1.3 %collective-permute-start.9 = (bf16[4,32,1024]{2,1,0:T(8,128)(2,1)S(1)}, bf16[4,32,1024]{2,1,0:T(8,128)(2,1)S(1)}, u32[]{:S(2)}, u32[]{:S(2)}) collective-permute-start(bf16[4,32,1024]{2,1,0:T(8,128)(2,1)S(1)} %pad_maximum_fusion.rest_5_), channel_id=1, source_target_pairs={{0,1},{2,3},{4,5},{6,7},{8,9},{10,11},{12,13},{14,15},{16,17},{18,... | collective-permute-start | bytes 786440 | tf_op jit(solution)/shard_map/ppermute | solution.py:504
  67.9 5.0 %collective-permute-done.4 = bf16[2,32,1024]{2,1,0:T(8,128)(2,1)S(1)} collective-permute-done((bf16[2,32,1024]{2,1,0:T(8,128)(2,1)S(1)}, bf16[2,32,1024]{2,1,0:T(8,128)(2,1)S(1)}, u32[]{:S(2)}, u32[]{:S(2)}) %collective-permute-start.4) | collective-permute-done | bytes 131104 | tf_op jit(solution)/shard_map/ppermute | solution.py:558
  72.9 3.4 %collective-permute-start.10 = (bf16[4,32,1024]{2,1,0:T(8,128)(2,1)S(1)}, bf16[4,32,1024]{2,1,0:T(8,128)(2,1)S(1)}, u32[]{:S(2)}, u32[]{:S(2)}) collective-permute-start(bf16[4,32,1024]{2,1,0:T(8,128)(2,1)S(1)} %constant_dynamic-update-slice_fusion.rest_6_), channel_id=1, source_target_pairs={{0,1},{2,3},{4,5},{6,7},{8,9},{10,11},{12,13},{14,15},{16,17},{18,... | collective-permute-start | bytes 786440 | tf_op jit(solution)/shard_map/ppermute | solution.py:504
  76.3 0.0 collective-permute-done.7.rest_8_
  76.3 1.3 %collective-permute-start.12 = (bf16[2,32,1024]{2,1,0:T(8,128)(2,1)}, bf16[2,32,1024]{2,1,0:T(8,128)(2,1)S(1)}, u32[]{:S(2)}, u32[]{:S(2)}) collective-permute-start(bf16[2,32,1024]{2,1,0:T(8,128)(2,1)} %collective-permute-done.7.rest_8_), channel_id=1, source_target_pairs={{0,1},{2,3},{4,5},{6,7},{8,9},{10,11},{12,13},{14,15},{16,17},{18,... | collective-permute-start | bytes 393224 | tf_op jit(solution)/shard_map/ppermute | solution.py:504
  77.6 0.0 collective-permute-done.8.rest_9_
  77.6 1.5 %collective-permute-start.13 = (bf16[2,32,1024]{2,1,0:T(8,128)(2,1)}, bf16[2,32,1024]{2,1,0:T(8,128)(2,1)S(1)}, u32[]{:S(2)}, u32[]{:S(2)}) collective-permute-start(bf16[2,32,1024]{2,1,0:T(8,128)(2,1)} %collective-permute-done.8.rest_9_), channel_id=1, source_target_pairs={{0,1},{2,3},{4,5},{6,7},{8,9},{10,11},{12,13},{14,15},{16,17},{18,... | collective-permute-start | bytes 393224 | tf_op jit(solution)/shard_map/ppermute | solution.py:504
  79.1 0.0 copy-done.1
  79.1 0.0 copy-done.2
  79.1 0.0 copy-done.3
  79.1 0.0 copy-done.4
  79.1 0.0 copy-done.5
  79.2 8.6 %late.2 = (f32[2,16,16384]{2,1,0:T(8,128)S(1)}, f32[2,16,16384]{2,1,0:T(8,128)}) custom-call(s32[1,1]{1,0:T(1,128)} %bitcast.me, f32[1,1]{1,0:T(1,128)} %bitcast.2.factor, f32[2,16,16384]{2,1,0:T(8,128)} %base.1, f32[16,16384]{1,0:T(8,128)S(1)} %copy-done.1, f32[2,128,128]{2,1,0:T(8,128)S(1)} %copy-done.4, bf16[256,256]{1,0:T(8,128)(2,1)S(1)} %copy-done.6, ...), custom_call_target="tpu_custom_call" | custom-call | tf_op jit(solution)/shard_map/late/pallas_call | solution.py:417
  87.8 0.0 collective-permute-done.12.rest_8_
  87.8 0.6 collective-permute-done.13.rest_9_
  88.4 0.0 collective-permute-done.11.rest_7_
  88.4 0.0 collective-permute-done.9.rest_5_
  88.4 0.0 collective-permute-done.10.rest_6_
  88.4 4.9 %late.3 = f32[2,16,16384]{2,1,0:T(8,128)} custom-call(s32[1,1]{1,0:T(1,128)} %bitcast.me, f32[1,1]{1,0:T(1,128)} %bitcast.1.factor, f32[2,16,16384]{2,1,0:T(8,128)S(1)} %get-tuple-element.41.base, f32[2,16,16384]{2,1,0:T(8,128)} %get-tuple-element.42.phase, f32[2,128,128]{2,1,0:T(8,128)S(1)} %copy-done.4, bf16[256,256]{1,0:T(8,128)(2,1)S(1)} %copy-done.6, ...), custom_call_target="tpu_custom_call" | custom-call | tf_op jit(solution)/shard_map/late/pallas_call | solution.py:417
  (11 shorter events, 0.1 us)
Async XLA Ops:
  7.3 7.6 %copy-start = (bf16[2048,256]{1,0:T(8,128)(2,1)S(1)}, bf16[2048,256]{1,0:T(8,128)(2,1)}, u32[]{:S(2)}) copy-start(bf16[2048,256]{1,0:T(8,128)(2,1)} %profiles.1) | copy-start | bytes 3145732
  7.3 30.4 %copy-start.7 = (f32[2048]{0:T(1024)S(1)}, f32[2048]{0:T(1024)}, u32[]{:S(2)}) copy-start(f32[2048]{0:T(1024)} %param.16) | copy-start | bytes 24580
  7.3 30.4 %all-to-all-start = ((bf16[16,32,1024]{2,1,0:T(8,128)(2,1)}), bf16[16,32,1024]{2,1,0:T(8,128)(2,1)S(1)}, u32[]{:S(2)}, u32[]{:S(2)}) async-start(bf16[16,32,1024]{2,1,0:T(8,128)(2,1)} %inverse.1), calls=%async_computation | async-start | bytes 2097152 | tf_op jit(solution)/shard_map/all_to_all | solution.py:547
  44.3 34.8 %copy-start.1 = (f32[16,16384]{1,0:T(8,128)S(1)}, f32[16,16384]{1,0:T(8,128)}, u32[]{:S(2)}) copy-start(f32[16,16384]{1,0:T(8,128)} %phase.3) | copy-start | bytes 3145732
  44.3 34.8 %copy-start.2 = (bf16[256,256]{1,0:T(8,128)(2,1)S(1)}, bf16[256,256]{1,0:T(8,128)(2,1)}, u32[]{:S(2)}) copy-start(bf16[256,256]{1,0:T(8,128)(2,1)} %constant.30.clone.rest_4_) | copy-start | bytes 393220
  44.3 34.8 %copy-start.3 = (bf16[256,256]{1,0:T(8,128)(2,1)S(1)}, bf16[256,256]{1,0:T(8,128)(2,1)}, u32[]{:S(2)}) copy-start(bf16[256,256]{1,0:T(8,128)(2,1)} %constant.29.clone.rest_3_) | copy-start | bytes 393220
  44.3 34.8 %copy-start.4 = (f32[2,128,128]{2,1,0:T(8,128)S(1)}, f32[2,128,128]{2,1,0:T(8,128)}, u32[]{:S(2)}) copy-start(f32[2,128,128]{2,1,0:T(8,128)} %constant.26.clone.rest_0_) | copy-start | bytes 393220
  44.3 34.8 %copy-start.5 = (bf16[256,256]{1,0:T(8,128)(2,1)S(1)}, bf16[256,256]{1,0:T(8,128)(2,1)}, u32[]{:S(2)}) copy-start(bf16[256,256]{1,0:T(8,128)(2,1)} %constant.32.clone.rest_2_) | copy-start | bytes 393220
  44.3 34.8 %copy-start.6 = (bf16[256,256]{1,0:T(8,128)(2,1)S(1)}, bf16[256,256]{1,0:T(8,128)(2,1)}, u32[]{:S(2)}) copy-start(bf16[256,256]{1,0:T(8,128)(2,1)} %constant.31.clone.rest_1_) | copy-start | bytes 393220
  44.3 1.9 %collective-permute-start = (bf16[4,32,1024]{2,1,0:T(8,128)(2,1)S(1)}, bf16[4,32,1024]{2,1,0:T(8,128)(2,1)S(1)}, u32[]{:S(2)}, u32[]{:S(2)}) collective-permute-start(bf16[4,32,1024]{2,1,0:T(8,128)(2,1)S(1)} %get-tuple-element.25), channel_id=1, source_target_pairs={{0,2},{2,0},{4,6},{6,4},{8,10},{10,8},{12,14},{14,12},{16,18},{18,... | collective-permute-start | bytes 786440 | tf_op jit(solution)/shard_map/ppermute | solution.py:553
  45.1 6.2 %collective-permute-start.2 = (bf16[4,32,1024]{2,1,0:T(8,128)(2,1)S(1)}, bf16[4,32,1024]{2,1,0:T(8,128)(2,1)S(1)}, u32[]{:S(2)}, u32[]{:S(2)}) collective-permute-start(bf16[4,32,1024]{2,1,0:T(8,128)(2,1)S(1)} %get-tuple-element.34), channel_id=1, source_target_pairs={{0,2},{2,0},{4,6},{6,4},{8,10},{10,8},{12,14},{14,12},{16,18},{18,... | collective-permute-start | bytes 786440 | tf_op jit(solution)/shard_map/ppermute | solution.py:552
  46.3 8.9 %collective-permute-start.5 = (bf16[2,32,1024]{2,1,0:T(8,128)(2,1)S(1)}, bf16[2,32,1024]{2,1,0:T(8,128)(2,1)S(1)}, u32[]{:S(2)}, u32[]{:S(2)}) collective-permute-start(bf16[2,32,1024]{2,1,0:T(8,128)(2,1)S(1)} %get-tuple-element.37), channel_id=1, source_target_pairs={{0,8},{2,10},{4,12},{6,14},{8,0},{10,2},{12,4},{14,6},{16,24},{18,... | collective-permute-start | bytes 393224 | tf_op jit(solution)/shard_map/ppermute | solution.py:558
  49.7 10.6 %collective-permute-start.6 = (bf16[2,32,1024]{2,1,0:T(8,128)(2,1)S(1)}, bf16[2,32,1024]{2,1,0:T(8,128)(2,1)S(1)}, u32[]{:S(2)}, u32[]{:S(2)}) collective-permute-start(bf16[2,32,1024]{2,1,0:T(8,128)(2,1)S(1)} %get-tuple-element.38), channel_id=1, source_target_pairs={{0,12},{2,14},{4,8},{6,10},{8,4},{10,6},{12,0},{14,2},{16,28},{18,... | collective-permute-start | bytes 393224 | tf_op jit(solution)/shard_map/ppermute | solution.py:558
  50.7 12.4 %collective-permute-start.1 = (bf16[2,32,1024]{2,1,0:T(8,128)(2,1)S(1)}, bf16[2,32,1024]{2,1,0:T(8,128)(2,1)S(1)}, u32[]{:S(2)}, u32[]{:S(2)}) collective-permute-start(bf16[2,32,1024]{2,1,0:T(8,128)(2,1)S(1)} %get-tuple-element.29), channel_id=1, source_target_pairs={{0,4},{2,6},{4,0},{6,2},{8,12},{10,14},{12,8},{14,10},{16,20},{18,... | collective-permute-start | bytes 393224 | tf_op jit(solution)/shard_map/ppermute | solution.py:558
  51.3 15.2 %collective-permute-start.3 = (bf16[2,32,1024]{2,1,0:T(8,128)(2,1)S(1)}, bf16[2,32,1024]{2,1,0:T(8,128)(2,1)S(1)}, u32[]{:S(2)}, u32[]{:S(2)}) collective-permute-start(bf16[2,32,1024]{2,1,0:T(8,128)(2,1)S(1)} %get-tuple-element.35), channel_id=1, source_target_pairs={{0,16},{2,18},{4,20},{6,22},{8,24},{10,26},{12,28},{14,30},{16,0},... | collective-permute-start | bytes 393224 | tf_op jit(solution)/shard_map/ppermute | solution.py:558
  54.7 18.1 %collective-permute-start.4 = (bf16[2,32,1024]{2,1,0:T(8,128)(2,1)S(1)}, bf16[2,32,1024]{2,1,0:T(8,128)(2,1)S(1)}, u32[]{:S(2)}, u32[]{:S(2)}) collective-permute-start(bf16[2,32,1024]{2,1,0:T(8,128)(2,1)S(1)} %get-tuple-element.36), channel_id=1, source_target_pairs={{0,20},{2,22},{4,16},{6,18},{8,28},{10,30},{12,24},{14,26},{16,4},... | collective-permute-start | bytes 393224 | tf_op jit(solution)/shard_map/ppermute | solution.py:558
  55.2 21.1 %collective-permute-start.7 = (bf16[2,32,1024]{2,1,0:T(8,128)(2,1)S(1)}, bf16[2,32,1024]{2,1,0:T(8,128)(2,1)}, u32[]{:S(2)}, u32[]{:S(2)}) collective-permute-start(bf16[2,32,1024]{2,1,0:T(8,128)(2,1)S(1)} %get-tuple-element.39), channel_id=1, source_target_pairs={{0,24},{2,26},{4,28},{6,30},{8,16},{10,18},{12,20},{14,22},{16,8},... | collective-permute-start | bytes 393224 | tf_op jit(solution)/shard_map/ppermute | solution.py:558
  60.3 17.3 %collective-permute-start.8 = (bf16[2,32,1024]{2,1,0:T(8,128)(2,1)S(1)}, bf16[2,32,1024]{2,1,0:T(8,128)(2,1)}, u32[]{:S(2)}, u32[]{:S(2)}) collective-permute-start(bf16[2,32,1024]{2,1,0:T(8,128)(2,1)S(1)} %get-tuple-element.40), channel_id=1, source_target_pairs={{0,28},{2,30},{4,24},{6,26},{8,20},{10,22},{12,16},{14,18},{16,12}... | collective-permute-start | bytes 393224 | tf_op jit(solution)/shard_map/ppermute | solution.py:558
  63.0 25.4 %collective-permute-start.11 = (bf16[4,32,1024]{2,1,0:T(8,128)(2,1)S(1)}, bf16[4,32,1024]{2,1,0:T(8,128)(2,1)S(1)}, u32[]{:S(2)}, u32[]{:S(2)}) collective-permute-start(bf16[4,32,1024]{2,1,0:T(8,128)(2,1)S(1)} %constant_dynamic-update-slice_fusion.2.rest_7_), channel_id=1, source_target_pairs={{0,1},{2,3},{4,5},{6,7},{8,9},{10,11},{12,13},{14,15},{16,17},{18,... | collective-permute-start | bytes 786440 | tf_op jit(solution)/shard_map/ppermute | solution.py:504
  66.5 21.9 %collective-permute-start.9 = (bf16[4,32,1024]{2,1,0:T(8,128)(2,1)S(1)}, bf16[4,32,1024]{2,1,0:T(8,128)(2,1)S(1)}, u32[]{:S(2)}, u32[]{:S(2)}) collective-permute-start(bf16[4,32,1024]{2,1,0:T(8,128)(2,1)S(1)} %pad_maximum_fusion.rest_5_), channel_id=1, source_target_pairs={{0,1},{2,3},{4,5},{6,7},{8,9},{10,11},{12,13},{14,15},{16,17},{18,... | collective-permute-start | bytes 786440 | tf_op jit(solution)/shard_map/ppermute | solution.py:504
  72.9 15.6 %collective-permute-start.10 = (bf16[4,32,1024]{2,1,0:T(8,128)(2,1)S(1)}, bf16[4,32,1024]{2,1,0:T(8,128)(2,1)S(1)}, u32[]{:S(2)}, u32[]{:S(2)}) collective-permute-start(bf16[4,32,1024]{2,1,0:T(8,128)(2,1)S(1)} %constant_dynamic-update-slice_fusion.rest_6_), channel_id=1, source_target_pairs={{0,1},{2,3},{4,5},{6,7},{8,9},{10,11},{12,13},{14,15},{16,17},{18,... | collective-permute-start | bytes 786440 | tf_op jit(solution)/shard_map/ppermute | solution.py:504
  76.3 11.5 %collective-permute-start.12 = (bf16[2,32,1024]{2,1,0:T(8,128)(2,1)}, bf16[2,32,1024]{2,1,0:T(8,128)(2,1)S(1)}, u32[]{:S(2)}, u32[]{:S(2)}) collective-permute-start(bf16[2,32,1024]{2,1,0:T(8,128)(2,1)} %collective-permute-done.7.rest_8_), channel_id=1, source_target_pairs={{0,1},{2,3},{4,5},{6,7},{8,9},{10,11},{12,13},{14,15},{16,17},{18,... | collective-permute-start | bytes 393224 | tf_op jit(solution)/shard_map/ppermute | solution.py:504
  77.6 10.8 %collective-permute-start.13 = (bf16[2,32,1024]{2,1,0:T(8,128)(2,1)}, bf16[2,32,1024]{2,1,0:T(8,128)(2,1)S(1)}, u32[]{:S(2)}, u32[]{:S(2)}) collective-permute-start(bf16[2,32,1024]{2,1,0:T(8,128)(2,1)} %collective-permute-done.8.rest_9_), channel_id=1, source_target_pairs={{0,1},{2,3},{4,5},{6,7},{8,9},{10,11},{12,13},{14,15},{16,17},{18,... | collective-permute-start | bytes 393224 | tf_op jit(solution)/shard_map/ppermute | solution.py:504

commit v4 on v3

--- a/solution.py
+++ b/solution.py
@@ -147,7 +147,7 @@
             for copy in copies[side * HALVES + at]:
                 copy.wait()
             part = radix // HALVES
-            lax.fori_loop(at * part, (at + 1) * part, rotate, 0, unroll=8)
+            lax.fori_loop(at * part, (at + 1) * part, rotate, 0, unroll=16)
         if side == 0:
             for copy in more:
                 copy.wait()
@@ -219,29 +219,16 @@
 def kerr_kernel(modes, devices, step, lanes, me, fields, profiles, flipped, weights, *rest):
     chips = devices // 2
     keeps, gives = rest[:chips], rest[chips : chips + 2]
-    gathered, fields_t, total_t, total, sems = rest[chips + 2 :]
-    points, _ = profiles.shape
+    fields_t, total_t, total = rest[chips + 2 :]
+    points = profiles.shape[0]
     width = fields.shape[-1]
     tiles = width // lanes
-    copies = []
     for tile in range(tiles):
         cut = slice(tile * lanes, (tile + 1) * lanes)
-        for source in range(devices):
-            for c in range(2):
-                copies.append(
-                    pltpu.make_async_copy(
-                        fields.at[source, c * modes : (c + 1) * modes, cut],
-                        gathered.at[c, source * modes : (source + 1) * modes, cut],
-                        sems.at[len(copies)],
-                    )
-                )
-                copies[-1].start()
-    for tile in range(tiles):
-        cut = slice(tile * lanes, (tile + 1) * lanes)
-        for copy in copies[tile * 2 * devices : (tile + 1) * 2 * devices]:
-            copy.wait()
         for c in range(2):
-            fields_t[c, cut, :] = gathered[c, :, cut].T
+            rows = slice(c * modes, (c + 1) * modes)
+            block = jnp.concatenate([fields[source, rows, cut] for source in range(devices)], 0)
+            fields_t[c, cut, :] = block.T
     for at in range(0, points, step):
         these = slice(at, at + step)
         for tile in range(tiles):
@@ -277,14 +264,12 @@
         functools.partial(kerr_kernel, modes, devices, KSTEP, KTILE),
         out_shape=[jax.ShapeDtypeStruct((2 * modes, width), bf16)] * chips
         + [jax.ShapeDtypeStruct((chips // 2, 2 * modes, width), bf16)] * 2,
-        in_specs=specs("savvv"),
+        in_specs=specs("svvvv"),
         out_specs=specs("v" * (chips + 2)),
         scratch_shapes=[
-            pltpu.VMEM((2, devices * modes, width), bf16),
             pltpu.VMEM((2, width, devices * modes), bf16),
             pltpu.VMEM((2, width, devices * modes), f32),
             pltpu.VMEM((2, devices * modes, width), f32),
-            pltpu.SemaphoreType.DMA((2 * devices * (width // KTILE),)),
         ],
         compiler_params=params(),
         name="kerr",
@@ -396,7 +381,7 @@
         part = radix // STRIPES
         if not first:
             inward[at].wait()
-        lax.fori_loop(at * part, (at + 1) * part, finish, 0, unroll=4)
+        lax.fori_loop(at * part, (at + 1) * part, finish, 0, unroll=8)
         if last:
             copies.append(
                 pltpu.make_async_copy(result.at[:, :, cut], out.at[:, :, cut], spare[1].at[at])

time: 93.8 us -> 92.2 us (0.983)
  Pallas kernels: 27.4 us -> 25.6 us
    pallas_call x1, Pallas kernels: 6.48 us -> 4.97 us  [kerr(): pl.pallas_call(functools.partial(kerr_kernel, modes, devices, KSTEP, KTIL...]
where the time goes in v4:
time: 92.2 us; the launch traced here: 91.9 us
  starting transfers between devices  33.8 us (37%)
  waiting for transfers between devices  31.3 us (34%)
  Pallas kernels  25.6 us (28%)
    all_to_all x1, waiting for transfers between devices, on_device(): fields = lax.all_to_all(fields, 'modes', 0, 0, tiled=True)  22.2 us
    ppermute x7, starting transfers between devices, on_device(): got[chip] = lax.ppermute(got[chip], 'modes', pairs)  14.4 us
    pallas_call x2, Pallas kernels, late(): pl.pallas_call(functools.partial(late_kernel, modes, devices, first, not...  13.3 us
    ppermute x5, starting transfers between devices, onward(): held.append(lax.ppermute(values, 'gz', pairs))  11 us
    all_to_all x1, starting transfers between devices, on_device(): fields = lax.all_to_all(fields, 'modes', 0, 0, tiled=True)  7.53 us
    pallas_call x1, Pallas kernels, inverse(): pl.pallas_call(functools.partial(inverse_kernel, modes, devices), out_sha...  7.23 us
    ppermute x7, waiting for transfers between devices, on_device(): got[chip] = lax.ppermute(got[chip], 'modes', pairs)  7.2 us
    pallas_call x1, Pallas kernels, kerr(): pl.pallas_call(functools.partial(kerr_kernel, modes, devices, KSTEP, KTIL...  4.97 us
  transfers between devices with their start and end apart: 15, of which 5 were waited for; matrix products, arithmetic and copies ran while one was open for 1% of the time, Pallas kernels for 9%

profile of v4, /device:TPU:0, one launch (start us, length us, event | category | flops | bytes accessed | tf_op | source)
XLA Modules:
  0.0 91.9 jit_solution(808515422872566309)
XLA Ops:
  0.0 7.2 %inverse.1 = bf16[16,32,1024]{2,1,0:T(8,128)(2,1)} custom-call(f32[1,1]{1,0:T(1,128)} %bitcast.2.factor, f32[2,16,16384]{2,1,0:T(8,128)} %base.1, f32[16,16384]{1,0:T(8,128)} %phase.3, f32[2,128,128]{2,1,0:T(8,128)} %constant.26.clone.rest_0_, bf16[256,256]{1,0:T(8,128)(2,1)} %constant.27.clone.rest_1_, bf16[256,256]{1,0:T(8,128)(2,1)} %constant.28.clone.rest_2_, ...), custom_call_target="tpu_custom_call" | custom-call | tf_op jit(solution)/shard_map/inverse/pallas_call | solution.py:194
  7.2 0.0 copy-start
  7.3 0.0 copy-start.7
  7.3 7.5 %all-to-all-start = ((bf16[16,32,1024]{2,1,0:T(8,128)(2,1)}), bf16[16,32,1024]{2,1,0:T(8,128)(2,1)S(1)}, u32[]{:S(2)}, u32[]{:S(2)}) async-start(bf16[16,32,1024]{2,1,0:T(8,128)(2,1)} %inverse.1), calls=%async_computation | async-start | bytes 2097152 | tf_op jit(solution)/shard_map/all_to_all | solution.py:532
  14.8 0.0 copy-done
  14.8 0.6 copy.14
  15.5 22.2 %all-to-all-done.fields = bf16[16,32,1024]{2,1,0:T(8,128)(2,1)S(1)} async-done(((bf16[16,32,1024]{2,1,0:T(8,128)(2,1)}), bf16[16,32,1024]{2,1,0:T(8,128)(2,1)S(1)}, u32[]{:S(2)}, u32[]{:S(2)}) %all-to-all-start) | async-done | bytes 1048608 | tf_op jit(solution)/shard_map/all_to_all | solution.py:532
  37.7 0.0 copy-done.7
  37.7 5.0 %kerr.1 = (bf16[32,1024]{1,0:T(8,128)(2,1)S(1)}, bf16[32,1024]{1,0:T(8,128)(2,1)S(1)}, bf16[32,1024]{1,0:T(8,128)(2,1)S(1)}, bf16[32,1024]{1,0:T(8,128)(2,1)S(1)...) custom-call(s32[1,1]{1,0:T(1,128)} %bitcast.me, ...), custom_call_target="tpu_custom_call" | custom-call | tf_op jit(solution)/shard_map/kerr/pallas_call | solution.py:263
  42.7 0.0 copy-start.1
  42.7 0.0 copy-start.2
  42.7 0.0 copy-start.3
  42.7 0.0 copy-start.4
  42.7 0.0 copy-start.5
  42.7 0.0 copy-start.6
  42.7 0.8 collective-permute-start
  43.5 0.1 collective-permute-start.2
  43.6 1.1 %collective-permute-done.refs_3_ = bf16[4,32,1024]{2,1,0:T(8,128)(2,1)S(1)} collective-permute-done((bf16[4,32,1024]{2,1,0:T(8,128)(2,1)S(1)}, bf16[4,32,1024]{2,1,0:T(8,128)(2,1)S(1)}, u32[]{:S(2)}, u32[]{:S(2)}) %collective-permute-start) | collective-permute-done | bytes 262176 | tf_op jit(solution)/shard_map/ppermute | solution.py:538
  44.7 3.4 %collective-permute-start.5 = (bf16[2,32,1024]{2,1,0:T(8,128)(2,1)S(1)}, bf16[2,32,1024]{2,1,0:T(8,128)(2,1)S(1)}, u32[]{:S(2)}, u32[]{:S(2)}) collective-permute-start(bf16[2,32,1024]{2,1,0:T(8,128)(2,1)S(1)} %get-tuple-element.37), channel_id=1, source_target_pairs={{0,8},{2,10},{4,12},{6,14},{8,0},{10,2},{12,4},{14,6},{16,24},{18,... | collective-permute-start | bytes 393224 | tf_op jit(solution)/shard_map/ppermute | solution.py:543
  48.1 0.9 collective-permute-start.6
  49.1 0.6 collective-permute-start.1
  49.7 0.0 collective-permute-done.2.refs_4_
  49.7 3.4 %collective-permute-start.3 = (bf16[2,32,1024]{2,1,0:T(8,128)(2,1)S(1)}, bf16[2,32,1024]{2,1,0:T(8,128)(2,1)S(1)}, u32[]{:S(2)}, u32[]{:S(2)}) collective-permute-start(bf16[2,32,1024]{2,1,0:T(8,128)(2,1)S(1)} %get-tuple-element.35), channel_id=1, source_target_pairs={{0,16},{2,18},{4,20},{6,22},{8,24},{10,26},{12,28},{14,30},{16,0},... | collective-permute-start | bytes 393224 | tf_op jit(solution)/shard_map/ppermute | solution.py:543
  53.1 0.4 collective-permute-start.4
  53.6 0.0 collective-permute-done.5
  53.6 2.9 %collective-permute-start.7 = (bf16[2,32,1024]{2,1,0:T(8,128)(2,1)S(1)}, bf16[2,32,1024]{2,1,0:T(8,128)(2,1)}, u32[]{:S(2)}, u32[]{:S(2)}) collective-permute-start(bf16[2,32,1024]{2,1,0:T(8,128)(2,1)S(1)} %get-tuple-element.39), channel_id=1, source_target_pairs={{0,24},{2,26},{4,28},{6,30},{8,16},{10,18},{12,20},{14,22},{16,8},... | collective-permute-start | bytes 393224 | tf_op jit(solution)/shard_map/ppermute | solution.py:543
  56.5 2.2 %collective-permute-done.6 = bf16[2,32,1024]{2,1,0:T(8,128)(2,1)S(1)} collective-permute-done((bf16[2,32,1024]{2,1,0:T(8,128)(2,1)S(1)}, bf16[2,32,1024]{2,1,0:T(8,128)(2,1)S(1)}, u32[]{:S(2)}, u32[]{:S(2)}) %collective-permute-start.6) | collective-permute-done | bytes 131104 | tf_op jit(solution)/shard_map/ppermute | solution.py:543
  58.7 2.7 %collective-permute-start.8 = (bf16[2,32,1024]{2,1,0:T(8,128)(2,1)S(1)}, bf16[2,32,1024]{2,1,0:T(8,128)(2,1)}, u32[]{:S(2)}, u32[]{:S(2)}) collective-permute-start(bf16[2,32,1024]{2,1,0:T(8,128)(2,1)S(1)} %get-tuple-element.40), channel_id=1, source_target_pairs={{0,28},{2,30},{4,24},{6,26},{8,20},{10,22},{12,16},{14,18},{16,12}... | collective-permute-start | bytes 393224 | tf_op jit(solution)/shard_map/ppermute | solution.py:543
  61.4 0.0 collective-permute-done.1
  61.4 3.4 %collective-permute-start.11 = (bf16[4,32,1024]{2,1,0:T(8,128)(2,1)S(1)}, bf16[4,32,1024]{2,1,0:T(8,128)(2,1)S(1)}, u32[]{:S(2)}, u32[]{:S(2)}) collective-permute-start(bf16[4,32,1024]{2,1,0:T(8,128)(2,1)S(1)} %constant_dynamic-update-slice_fusion.2.rest_7_), channel_id=1, source_target_pairs={{0,1},{2,3},{4,5},{6,7},{8,9},{10,11},{12,13},{14,15},{16,17},{18,... | collective-permute-start | bytes 786440 | tf_op jit(solution)/shard_map/ppermute | solution.py:489
  64.9 0.0 collective-permute-done.3
  64.9 1.3 %collective-permute-start.9 = (bf16[4,32,1024]{2,1,0:T(8,128)(2,1)S(1)}, bf16[4,32,1024]{2,1,0:T(8,128)(2,1)S(1)}, u32[]{:S(2)}, u32[]{:S(2)}) collective-permute-start(bf16[4,32,1024]{2,1,0:T(8,128)(2,1)S(1)} %pad_maximum_fusion.rest_5_), channel_id=1, source_target_pairs={{0,1},{2,3},{4,5},{6,7},{8,9},{10,11},{12,13},{14,15},{16,17},{18,... | collective-permute-start | bytes 786440 | tf_op jit(solution)/shard_map/ppermute | solution.py:489
  66.3 5.0 %collective-permute-done.4 = bf16[2,32,1024]{2,1,0:T(8,128)(2,1)S(1)} collective-permute-done((bf16[2,32,1024]{2,1,0:T(8,128)(2,1)S(1)}, bf16[2,32,1024]{2,1,0:T(8,128)(2,1)S(1)}, u32[]{:S(2)}, u32[]{:S(2)}) %collective-permute-start.4) | collective-permute-done | bytes 131104 | tf_op jit(solution)/shard_map/ppermute | solution.py:543
  71.2 3.4 %collective-permute-start.10 = (bf16[4,32,1024]{2,1,0:T(8,128)(2,1)S(1)}, bf16[4,32,1024]{2,1,0:T(8,128)(2,1)S(1)}, u32[]{:S(2)}, u32[]{:S(2)}) collective-permute-start(bf16[4,32,1024]{2,1,0:T(8,128)(2,1)S(1)} %constant_dynamic-update-slice_fusion.rest_6_), channel_id=1, source_target_pairs={{0,1},{2,3},{4,5},{6,7},{8,9},{10,11},{12,13},{14,15},{16,17},{18,... | collective-permute-start | bytes 786440 | tf_op jit(solution)/shard_map/ppermute | solution.py:489
  74.7 0.0 collective-permute-done.7.rest_8_
  74.7 1.3 %collective-permute-start.12 = (bf16[2,32,1024]{2,1,0:T(8,128)(2,1)}, bf16[2,32,1024]{2,1,0:T(8,128)(2,1)S(1)}, u32[]{:S(2)}, u32[]{:S(2)}) collective-permute-start(bf16[2,32,1024]{2,1,0:T(8,128)(2,1)} %collective-permute-done.7.rest_8_), channel_id=1, source_target_pairs={{0,1},{2,3},{4,5},{6,7},{8,9},{10,11},{12,13},{14,15},{16,17},{18,... | collective-permute-start | bytes 393224 | tf_op jit(solution)/shard_map/ppermute | solution.py:489
  76.0 0.0 collective-permute-done.8.rest_9_
  76.0 1.5 %collective-permute-start.13 = (bf16[2,32,1024]{2,1,0:T(8,128)(2,1)}, bf16[2,32,1024]{2,1,0:T(8,128)(2,1)S(1)}, u32[]{:S(2)}, u32[]{:S(2)}) collective-permute-start(bf16[2,32,1024]{2,1,0:T(8,128)(2,1)} %collective-permute-done.8.rest_9_), channel_id=1, source_target_pairs={{0,1},{2,3},{4,5},{6,7},{8,9},{10,11},{12,13},{14,15},{16,17},{18,... | collective-permute-start | bytes 393224 | tf_op jit(solution)/shard_map/ppermute | solution.py:489
  77.5 0.0 copy-done.1
  77.5 0.0 copy-done.2
  77.5 0.0 copy-done.3
  77.6 8.5 %late.2 = (f32[2,16,16384]{2,1,0:T(8,128)S(1)}, f32[2,16,16384]{2,1,0:T(8,128)}) custom-call(s32[1,1]{1,0:T(1,128)} %bitcast.me, f32[1,1]{1,0:T(1,128)} %bitcast.2.factor, f32[2,16,16384]{2,1,0:T(8,128)} %base.1, f32[16,16384]{1,0:T(8,128)S(1)} %copy-done.1, f32[2,128,128]{2,1,0:T(8,128)S(1)} %copy-done.4, bf16[256,256]{1,0:T(8,128)(2,1)S(1)} %copy-done.6, ...), custom_call_target="tpu_custom_call" | custom-call | tf_op jit(solution)/shard_map/late/pallas_call | solution.py:402
  86.1 0.0 collective-permute-done.12.rest_8_
  86.1 0.8 collective-permute-done.13.rest_9_
  86.8 0.0 collective-permute-done.11.rest_7_
  86.8 0.0 collective-permute-done.9.rest_5_
  86.8 0.0 collective-permute-done.10.rest_6_
  86.8 4.9 %late.3 = f32[2,16,16384]{2,1,0:T(8,128)} custom-call(s32[1,1]{1,0:T(1,128)} %bitcast.me, f32[1,1]{1,0:T(1,128)} %bitcast.1.factor, f32[2,16,16384]{2,1,0:T(8,128)S(1)} %get-tuple-element.41.base, f32[2,16,16384]{2,1,0:T(8,128)} %get-tuple-element.42.phase, f32[2,128,128]{2,1,0:T(8,128)S(1)} %copy-done.4, bf16[256,256]{1,0:T(8,128)(2,1)S(1)} %copy-done.6, ...), custom_call_target="tpu_custom_call" | custom-call | tf_op jit(solution)/shard_map/late/pallas_call | solution.py:402
  (11 shorter events, 0.1 us)
Async XLA Ops:
  7.2 7.6 %copy-start = (bf16[2048,256]{1,0:T(8,128)(2,1)S(1)}, bf16[2048,256]{1,0:T(8,128)(2,1)}, u32[]{:S(2)}) copy-start(bf16[2048,256]{1,0:T(8,128)(2,1)} %profiles.1) | copy-start | bytes 3145732
  7.3 30.4 %copy-start.7 = (f32[2048]{0:T(1024)S(1)}, f32[2048]{0:T(1024)}, u32[]{:S(2)}) copy-start(f32[2048]{0:T(1024)} %param.16) | copy-start | bytes 24580
  7.3 30.4 %all-to-all-start = ((bf16[16,32,1024]{2,1,0:T(8,128)(2,1)}), bf16[16,32,1024]{2,1,0:T(8,128)(2,1)S(1)}, u32[]{:S(2)}, u32[]{:S(2)}) async-start(bf16[16,32,1024]{2,1,0:T(8,128)(2,1)} %inverse.1), calls=%async_computation | async-start | bytes 2097152 | tf_op jit(solution)/shard_map/all_to_all | solution.py:532
  42.7 34.8 %copy-start.1 = (f32[16,16384]{1,0:T(8,128)S(1)}, f32[16,16384]{1,0:T(8,128)}, u32[]{:S(2)}) copy-start(f32[16,16384]{1,0:T(8,128)} %phase.3) | copy-start | bytes 3145732
  42.7 34.8 %copy-start.2 = (bf16[256,256]{1,0:T(8,128)(2,1)S(1)}, bf16[256,256]{1,0:T(8,128)(2,1)}, u32[]{:S(2)}) copy-start(bf16[256,256]{1,0:T(8,128)(2,1)} %constant.30.clone.rest_4_) | copy-start | bytes 393220
  42.7 34.8 %copy-start.3 = (bf16[256,256]{1,0:T(8,128)(2,1)S(1)}, bf16[256,256]{1,0:T(8,128)(2,1)}, u32[]{:S(2)}) copy-start(bf16[256,256]{1,0:T(8,128)(2,1)} %constant.29.clone.rest_3_) | copy-start | bytes 393220
  42.7 34.8 %copy-start.4 = (f32[2,128,128]{2,1,0:T(8,128)S(1)}, f32[2,128,128]{2,1,0:T(8,128)}, u32[]{:S(2)}) copy-start(f32[2,128,128]{2,1,0:T(8,128)} %constant.26.clone.rest_0_) | copy-start | bytes 393220
  42.7 34.8 %copy-start.5 = (bf16[256,256]{1,0:T(8,128)(2,1)S(1)}, bf16[256,256]{1,0:T(8,128)(2,1)}, u32[]{:S(2)}) copy-start(bf16[256,256]{1,0:T(8,128)(2,1)} %constant.32.clone.rest_2_) | copy-start | bytes 393220
  42.7 34.8 %copy-start.6 = (bf16[256,256]{1,0:T(8,128)(2,1)S(1)}, bf16[256,256]{1,0:T(8,128)(2,1)}, u32[]{:S(2)}) copy-start(bf16[256,256]{1,0:T(8,128)(2,1)} %constant.31.clone.rest_1_) | copy-start | bytes 393220
  42.7 1.9 %collective-permute-start = (bf16[4,32,1024]{2,1,0:T(8,128)(2,1)S(1)}, bf16[4,32,1024]{2,1,0:T(8,128)(2,1)S(1)}, u32[]{:S(2)}, u32[]{:S(2)}) collective-permute-start(bf16[4,32,1024]{2,1,0:T(8,128)(2,1)S(1)} %get-tuple-element.25), channel_id=1, source_target_pairs={{0,2},{2,0},{4,6},{6,4},{8,10},{10,8},{12,14},{14,12},{16,18},{18,... | collective-permute-start | bytes 786440 | tf_op jit(solution)/shard_map/ppermute | solution.py:538
  43.5 6.2 %collective-permute-start.2 = (bf16[4,32,1024]{2,1,0:T(8,128)(2,1)S(1)}, bf16[4,32,1024]{2,1,0:T(8,128)(2,1)S(1)}, u32[]{:S(2)}, u32[]{:S(2)}) collective-permute-start(bf16[4,32,1024]{2,1,0:T(8,128)(2,1)S(1)} %get-tuple-element.34), channel_id=1, source_target_pairs={{0,2},{2,0},{4,6},{6,4},{8,10},{10,8},{12,14},{14,12},{16,18},{18,... | collective-permute-start | bytes 786440 | tf_op jit(solution)/shard_map/ppermute | solution.py:537
  44.7 8.9 %collective-permute-start.5 = (bf16[2,32,1024]{2,1,0:T(8,128)(2,1)S(1)}, bf16[2,32,1024]{2,1,0:T(8,128)(2,1)S(1)}, u32[]{:S(2)}, u32[]{:S(2)}) collective-permute-start(bf16[2,32,1024]{2,1,0:T(8,128)(2,1)S(1)} %get-tuple-element.37), channel_id=1, source_target_pairs={{0,8},{2,10},{4,12},{6,14},{8,0},{10,2},{12,4},{14,6},{16,24},{18,... | collective-permute-start | bytes 393224 | tf_op jit(solution)/shard_map/ppermute | solution.py:543
  48.1 10.6 %collective-permute-start.6 = (bf16[2,32,1024]{2,1,0:T(8,128)(2,1)S(1)}, bf16[2,32,1024]{2,1,0:T(8,128)(2,1)S(1)}, u32[]{:S(2)}, u32[]{:S(2)}) collective-permute-start(bf16[2,32,1024]{2,1,0:T(8,128)(2,1)S(1)} %get-tuple-element.38), channel_id=1, source_target_pairs={{0,12},{2,14},{4,8},{6,10},{8,4},{10,6},{12,0},{14,2},{16,28},{18,... | collective-permute-start | bytes 393224 | tf_op jit(solution)/shard_map/ppermute | solution.py:543
  49.1 12.4 %collective-permute-start.1 = (bf16[2,32,1024]{2,1,0:T(8,128)(2,1)S(1)}, bf16[2,32,1024]{2,1,0:T(8,128)(2,1)S(1)}, u32[]{:S(2)}, u32[]{:S(2)}) collective-permute-start(bf16[2,32,1024]{2,1,0:T(8,128)(2,1)S(1)} %get-tuple-element.29), channel_id=1, source_target_pairs={{0,4},{2,6},{4,0},{6,2},{8,12},{10,14},{12,8},{14,10},{16,20},{18,... | collective-permute-start | bytes 393224 | tf_op jit(solution)/shard_map/ppermute | solution.py:543
  49.7 15.2 %collective-permute-start.3 = (bf16[2,32,1024]{2,1,0:T(8,128)(2,1)S(1)}, bf16[2,32,1024]{2,1,0:T(8,128)(2,1)S(1)}, u32[]{:S(2)}, u32[]{:S(2)}) collective-permute-start(bf16[2,32,1024]{2,1,0:T(8,128)(2,1)S(1)} %get-tuple-element.35), channel_id=1, source_target_pairs={{0,16},{2,18},{4,20},{6,22},{8,24},{10,26},{12,28},{14,30},{16,0},... | collective-permute-start | bytes 393224 | tf_op jit(solution)/shard_map/ppermute | solution.py:543
  53.1 18.1 %collective-permute-start.4 = (bf16[2,32,1024]{2,1,0:T(8,128)(2,1)S(1)}, bf16[2,32,1024]{2,1,0:T(8,128)(2,1)S(1)}, u32[]{:S(2)}, u32[]{:S(2)}) collective-permute-start(bf16[2,32,1024]{2,1,0:T(8,128)(2,1)S(1)} %get-tuple-element.36), channel_id=1, source_target_pairs={{0,20},{2,22},{4,16},{6,18},{8,28},{10,30},{12,24},{14,26},{16,4},... | collective-permute-start | bytes 393224 | tf_op jit(solution)/shard_map/ppermute | solution.py:543
  53.6 21.1 %collective-permute-start.7 = (bf16[2,32,1024]{2,1,0:T(8,128)(2,1)S(1)}, bf16[2,32,1024]{2,1,0:T(8,128)(2,1)}, u32[]{:S(2)}, u32[]{:S(2)}) collective-permute-start(bf16[2,32,1024]{2,1,0:T(8,128)(2,1)S(1)} %get-tuple-element.39), channel_id=1, source_target_pairs={{0,24},{2,26},{4,28},{6,30},{8,16},{10,18},{12,20},{14,22},{16,8},... | collective-permute-start | bytes 393224 | tf_op jit(solution)/shard_map/ppermute | solution.py:543
  58.7 17.3 %collective-permute-start.8 = (bf16[2,32,1024]{2,1,0:T(8,128)(2,1)S(1)}, bf16[2,32,1024]{2,1,0:T(8,128)(2,1)}, u32[]{:S(2)}, u32[]{:S(2)}) collective-permute-start(bf16[2,32,1024]{2,1,0:T(8,128)(2,1)S(1)} %get-tuple-element.40), channel_id=1, source_target_pairs={{0,28},{2,30},{4,24},{6,26},{8,20},{10,22},{12,16},{14,18},{16,12}... | collective-permute-start | bytes 393224 | tf_op jit(solution)/shard_map/ppermute | solution.py:543
  61.4 25.4 %collective-permute-start.11 = (bf16[4,32,1024]{2,1,0:T(8,128)(2,1)S(1)}, bf16[4,32,1024]{2,1,0:T(8,128)(2,1)S(1)}, u32[]{:S(2)}, u32[]{:S(2)}) collective-permute-start(bf16[4,32,1024]{2,1,0:T(8,128)(2,1)S(1)} %constant_dynamic-update-slice_fusion.2.rest_7_), channel_id=1, source_target_pairs={{0,1},{2,3},{4,5},{6,7},{8,9},{10,11},{12,13},{14,15},{16,17},{18,... | collective-permute-start | bytes 786440 | tf_op jit(solution)/shard_map/ppermute | solution.py:489
  64.9 21.9 %collective-permute-start.9 = (bf16[4,32,1024]{2,1,0:T(8,128)(2,1)S(1)}, bf16[4,32,1024]{2,1,0:T(8,128)(2,1)S(1)}, u32[]{:S(2)}, u32[]{:S(2)}) collective-permute-start(bf16[4,32,1024]{2,1,0:T(8,128)(2,1)S(1)} %pad_maximum_fusion.rest_5_), channel_id=1, source_target_pairs={{0,1},{2,3},{4,5},{6,7},{8,9},{10,11},{12,13},{14,15},{16,17},{18,... | collective-permute-start | bytes 786440 | tf_op jit(solution)/shard_map/ppermute | solution.py:489
  71.2 15.6 %collective-permute-start.10 = (bf16[4,32,1024]{2,1,0:T(8,128)(2,1)S(1)}, bf16[4,32,1024]{2,1,0:T(8,128)(2,1)S(1)}, u32[]{:S(2)}, u32[]{:S(2)}) collective-permute-start(bf16[4,32,1024]{2,1,0:T(8,128)(2,1)S(1)} %constant_dynamic-update-slice_fusion.rest_6_), channel_id=1, source_target_pairs={{0,1},{2,3},{4,5},{6,7},{8,9},{10,11},{12,13},{14,15},{16,17},{18,... | collective-permute-start | bytes 786440 | tf_op jit(solution)/shard_map/ppermute | solution.py:489
  74.7 11.4 %collective-permute-start.12 = (bf16[2,32,1024]{2,1,0:T(8,128)(2,1)}, bf16[2,32,1024]{2,1,0:T(8,128)(2,1)S(1)}, u32[]{:S(2)}, u32[]{:S(2)}) collective-permute-start(bf16[2,32,1024]{2,1,0:T(8,128)(2,1)} %collective-permute-done.7.rest_8_), channel_id=1, source_target_pairs={{0,1},{2,3},{4,5},{6,7},{8,9},{10,11},{12,13},{14,15},{16,17},{18,... | collective-permute-start | bytes 393224 | tf_op jit(solution)/shard_map/ppermute | solution.py:489
  76.0 10.8 %collective-permute-start.13 = (bf16[2,32,1024]{2,1,0:T(8,128)(2,1)}, bf16[2,32,1024]{2,1,0:T(8,128)(2,1)S(1)}, u32[]{:S(2)}, u32[]{:S(2)}) collective-permute-start(bf16[2,32,1024]{2,1,0:T(8,128)(2,1)} %collective-permute-done.8.rest_9_), channel_id=1, source_target_pairs={{0,1},{2,3},{4,5},{6,7},{8,9},{10,11},{12,13},{14,15},{16,17},{18,... | collective-permute-start | bytes 393224 | tf_op jit(solution)/shard_map/ppermute | solution.py:489
